TPU v7x, 256 devices: a whole 4x4x8 slice. The times are simulated.
256 devices in a mesh: ctx: 64 (over x, y_hi, z), tp: 4 (over y_lo, core).
Axes of the slice: x: 4, y: 4 (y_hi: 2, y_lo: 2; y = y_hi * 2 + y_lo), z: 8, core: 2. Of those that a mesh axis runs over, the one named last changes fastest.
Arguments:
- query_pre: bfloat16 [8192, 4096], P('ctx', 'tp'), may hold values from -6 to 6
- key_pre: bfloat16 [8192, 4096], P('ctx', 'tp'), may hold values from -6 to 6
- value_pre: bfloat16 [8192, 4096], P('ctx', 'tp'), may hold values from -6 to 6
- grad_out: bfloat16 [8192, 4096], P('ctx', 'tp'), may hold values from -6 to 6
- w_value: bfloat16 [4096, 4096], P(None, 'tp'), may hold values from -0.09375 to 0.09375
- short_taps: float32 [4096, 3, 3], P('tp'), may hold values from -3 to 3
- residues: float32 [4096, 16], P('tp'), may hold values from -0.3 to 0.3
- decay_rates: float32 [4096, 16], P('tp'), may hold values from 2.4414062e-06 to 0.05
- skip: float32 [4096], P('tp'), may hold values from -3 to 3
Outputs:
- input_grad: bfloat16 [8192, 4096], P(('ctx', 'tp'))
- query_grad: bfloat16 [8192, 4096], P('ctx', 'tp')
- key_grad: bfloat16 [8192, 4096], P('ctx', 'tp')
- d_residues: float32 [4096, 16], P('tp')
- d_skip: float32 [4096], P('tp')
- d_taps: float32 [4096, 3, 3], P('tp')
All inputs are finite; a program needn't handle non-finite values.
Results may differ from a plain program's by a relative error of at most 0.009.
Values may be sent and summed in bfloat16 or wider, within the bound.
A program may use at most 128 MiB of HBM per device.

v0:
```python
import jax
import jax.numpy as jnp
from jax import lax
from jax.sharding import PartitionSpec as P

highest = lax.Precision.HIGHEST


def compose(earlier, later):
    return (earlier[0] * later[0], later[0] * earlier[1] + later[1])


def modal_states(signal, rate_table):
    channels, length = signal.shape
    mode_count = rate_table.shape[1]
    block_len = min(128, length)
    blocks = length // block_len
    offsets = jnp.arange(block_len, dtype=jnp.float32)
    growth = jnp.exp(rate_table[:, :, None] * offsets)
    shrink = jnp.exp(-rate_table[:, :, None] * offsets)
    lifted = signal.reshape(channels, 1, blocks, block_len) * growth[:, :, None, :]
    triangle = (offsets[None, :] <= offsets[:, None]).astype(jnp.float32)
    inside = (
        jnp.einsum("cnks,ts->cnkt", lifted, triangle, precision=highest) * shrink[:, :, None, :]
    )
    block_decay = jnp.exp(-rate_table * block_len)
    span_table = jnp.broadcast_to(block_decay[:, :, None], inside.shape[:3])
    factor, block_ends = lax.associative_scan(compose, (span_table, inside[..., -1]), axis=2)
    before = jnp.concatenate([jnp.zeros_like(block_ends[..., :1]), block_ends[..., :-1]], axis=2)
    carried_in = (
        jnp.exp(-rate_table[:, :, None] * (offsets + 1.0))[:, :, None, :] * before[..., None]
    )
    states = inside + carried_in
    return (states.reshape(channels, mode_count, length), block_ends[..., -1])


def short_forward(streams, tap_table, history):
    tap_count = tap_table.shape[-1]
    length = streams.shape[-1]
    extended = jnp.concatenate([history, streams], axis=-1)
    summed = jnp.zeros_like(streams)
    for tap_index in range(tap_count):
        begin_at = tap_count - 1 - tap_index
        summed = (
            summed
            + tap_table[..., tap_index : tap_index + 1]
            * extended[..., begin_at : begin_at + length]
        )
    return (summed, extended)


def short_backward(stream_grads, tap_table, future):
    tap_count = tap_table.shape[-1]
    length = stream_grads.shape[-1]
    extended = jnp.concatenate([stream_grads, future], axis=-1)
    summed = jnp.zeros_like(stream_grads)
    for tap_index in range(tap_count):
        summed = (
            summed
            + tap_table[..., tap_index : tap_index + 1]
            * extended[..., tap_index : tap_index + length]
        )
    return summed


def tap_grads(stream_grads, extended, tap_count):
    length = stream_grads.shape[-1]
    columns = []
    for tap_index in range(tap_count):
        begin_at = tap_count - 1 - tap_index
        columns.append(jnp.sum(stream_grads * extended[..., begin_at : begin_at + length], axis=-1))
    return jnp.stack(columns, axis=-1)


def blocked_backward(pres, cotangent, taps, residue_table, rate_table, skip_table):
    tap_count = taps.shape[-1]
    chans, length = cotangent.shape
    block_len = min(128, length)
    blocks = length // block_len

    def delayed(values_in, amount):
        return jnp.pad(values_in, ((0, 0), (amount, 0)))[:, :length]

    def advance(values_in, amount):
        return jnp.pad(values_in, ((0, 0), (0, amount)))[:, amount:]

    feats = []
    for m in range(3):
        acc = taps[m][:, 0:1] * pres[m]
        for j in range(1, tap_count):
            acc = acc + taps[m][:, j : j + 1] * delayed(pres[m], j)
        feats.append(acc)
    query_feat, key_feat, value_feat = feats
    mixed = key_feat * value_feat
    grad_conv = cotangent * query_feat

    rate = rate_table[:, :, None]
    offs = jnp.arange(block_len, dtype=jnp.float32)
    up = jnp.exp(-rate * offs)
    down = jnp.exp(rate * offs)
    tri = (offs[:, None] <= offs[None, :]).astype(jnp.float32)
    toeplitz = (
        jnp.einsum("cns,cnt->cst", residue_table[:, :, None] * down, up, precision=highest) * tri
    )
    xb = mixed.reshape(chans, blocks, block_len)
    gb = grad_conv.reshape(chans, blocks, block_len)

    idx = jnp.arange(blocks, dtype=jnp.float32)
    gap = idx[:, None] - 1.0 - idx[None, :]
    carry_mat = jnp.where(
        gap >= 0, jnp.exp(-rate[..., None] * block_len * jnp.maximum(gap, 0.0)), 0.0
    )

    conv_intra = jnp.einsum("cks,cst->ckt", xb, toeplitz, precision=highest)
    tail_w = jnp.exp(-rate * (block_len - 1 - offs))
    ends = jnp.einsum("cks,cns->cnk", xb, tail_w, precision=highest)
    carried = jnp.einsum("cnkj,cnj->cnk", carry_mat, ends, precision=highest)
    lead_w = residue_table[:, :, None] * jnp.exp(-rate * (offs + 1.0))
    conv_carry = jnp.einsum("cnk,cnt->ckt", carried, lead_w, precision=highest)
    conv_out = (conv_intra + conv_carry).reshape(chans, length)

    back_intra = jnp.einsum("ckt,cst->cks", gb, toeplitz, precision=highest)
    starts = jnp.einsum("ckt,cnt->cnk", gb, up, precision=highest)
    later = jnp.einsum("cnjk,cnj->cnk", carry_mat, starts, precision=highest)
    back_w = jnp.exp(-rate * (block_len - offs))
    back_carry = jnp.einsum(
        "cnk,cns->cks", later, residue_table[:, :, None] * back_w, precision=highest
    )
    grad_mixed = (back_intra + back_carry).reshape(chans, length) + skip_table[:, None] * grad_conv

    pairs = jnp.einsum("cks,ckt->cst", xb, gb, precision=highest) * tri
    paired = jnp.einsum("cst,cnt->cns", pairs, up, precision=highest)
    res_intra = jnp.sum(paired * down, axis=2)
    lead_sums = jnp.einsum("cks,cns->cnk", xb, back_w, precision=highest)
    grad_residues = res_intra + jnp.sum(later * lead_sums, axis=2)
    grad_skip = jnp.sum(grad_conv * mixed, axis=1)

    grad_query = cotangent * (conv_out + skip_table[:, None] * mixed)
    stream_grads = (grad_query, grad_mixed * value_feat, grad_mixed * key_feat)
    pre_grads = []
    tap_cols = []
    for m in range(3):
        acc = taps[m][:, 0:1] * stream_grads[m]
        for j in range(1, tap_count):
            acc = acc + taps[m][:, j : j + 1] * advance(stream_grads[m], j)
        pre_grads.append(acc)
        tap_cols.append(
            jnp.stack(
                [jnp.sum(stream_grads[m] * delayed(pres[m], j), axis=1) for j in range(tap_count)],
                axis=-1,
            )
        )
    return (jnp.stack(pre_grads), grad_residues, grad_skip, jnp.stack(tap_cols))


def on_device(
    query_pre, key_pre, value_pre, grad_out, w_value, short_taps, residues, decay_rates, skip
):
    tap_count = short_taps.shape[2]
    stacked_in = jnp.stack([query_pre.T, key_pre.T, value_pre.T, grad_out.T])
    gathered_in = lax.all_to_all(stacked_in, "ctx", split_axis=1, concat_axis=2, tiled=True)
    regrouped = (gathered_in[0], gathered_in[1], gathered_in[2], gathered_in[3])
    local_chans = regrouped[0].shape[0]
    begin_at = lax.axis_index("ctx") * local_chans

    def own_rows(table):
        return lax.dynamic_slice_in_dim(table, begin_at, local_chans, 0)

    taps_here = jnp.transpose(own_rows(short_taps), (1, 0, 2))
    pre_grads, part_residues, part_skip, part_taps = blocked_backward(
        (
            regrouped[0].astype(jnp.float32),
            regrouped[1].astype(jnp.float32),
            regrouped[2].astype(jnp.float32),
        ),
        regrouped[3].astype(jnp.float32),
        taps_here,
        own_rows(residues),
        own_rows(decay_rates),
        own_rows(skip),
    )
    rounded = pre_grads.astype(jnp.bfloat16)
    returned = lax.all_to_all(rounded, "ctx", split_axis=2, concat_axis=1, tiled=True)
    query_grad = returned[0].T
    key_grad = returned[1].T
    value_grad = returned[2].T
    owners = lax.axis_size("ctx")
    local_rows = part_residues.shape[0]
    packed = jnp.concatenate(
        [
            part_residues,
            part_skip[:, None],
            jnp.transpose(part_taps, (1, 0, 2)).reshape(local_rows, -1),
        ],
        axis=1,
    )
    spread = jnp.broadcast_to(packed[None], (owners,) + packed.shape)
    everyone = lax.all_to_all(spread, "ctx", split_axis=0, concat_axis=0, tiled=True)
    everyone = everyone.reshape(owners * local_rows, packed.shape[1])
    mode_count = part_residues.shape[1]
    d_residues = everyone[:, :mode_count]
    d_skip = everyone[:, mode_count]
    d_taps = everyone[:, mode_count + 1 :].reshape(-1, part_taps.shape[0], tap_count)
    partial_sum = lax.dot_general(
        value_grad, w_value, (((1,), (1,)), ((), ())), preferred_element_type=jnp.float32
    )
    narrowed = lax.optimization_barrier(partial_sum.astype(jnp.bfloat16))
    input_grad = lax.psum_scatter(
        narrowed.astype(jnp.float32).astype(jnp.bfloat16), "tp", scatter_dimension=0, tiled=True
    )
    return (input_grad, query_grad, key_grad, d_residues, d_skip, d_taps)


def solution(mesh):
    in_specs = (
        P("ctx", "tp"),
        P("ctx", "tp"),
        P("ctx", "tp"),
        P("ctx", "tp"),
        P(None, "tp"),
        P("tp", None, None),
        P("tp", None),
        P("tp", None),
        P("tp"),
    )
    out_specs = (
        P(("ctx", "tp"), None),
        P("ctx", "tp"),
        P("ctx", "tp"),
        P("tp", None),
        P("tp"),
        P("tp", None, None),
    )
    return jax.shard_map(
        on_device, mesh=mesh, in_specs=in_specs, out_specs=out_specs, check_vma=False
    )
```

profile of v0, /device:TPU:8, one launch (start us, length us, event | category | flops | bytes accessed | tf_op | source)
XLA Modules:
  0.0 211.2 jit_solution(4878253107575466397)
XLA Ops:
  7.2 1.1 copy.74
  8.3 1.1 copy.75
  9.4 1.1 copy.76
  10.6 1.1 copy.77
  11.7 0.1 pad_maximum_fusion
  11.8 1.8 copy.78
  13.6 13.7 %all-to-all-start = ((bf16[4,1024,128]{2,0,1:T(4,128)(2,1)}), bf16[4,1024,128]{2,0,1:T(4,128)(2,1)S(1)}, u32[]{:S(2)}, u32[]{:S(2)}) async-start(bf16[4,1024,128]{2,0,1:T(4,128)(2,1)} %copy.78), calls=%async_computation | async-start | bytes 2097152 | tf_op jit(solution)/shard_map/all_to_all | solution.py:161
  27.3 0.2 reduce-scatter.2.cloned.1.call-start
  27.5 0.8 broadcast_multiply_fusion
  28.4 0.8 dynamic_slice.15
  29.4 0.1 dynamic-slice_bitcast_fusion
  29.7 1.9 convolution_multiply_fusion.1
  31.7 26.1 %all-to-all-done = bf16[4,1024,128]{2,0,1:T(4,128)(2,1)S(1)} async-done(((bf16[4,1024,128]{2,0,1:T(4,128)(2,1)}), bf16[4,1024,128]{2,0,1:T(4,128)(2,1)S(1)}, u32[]{:S(2)}, u32[]{:S(2)}) %all-to-all-start) | async-done | bytes 1048608 | tf_op jit(solution)/shard_map/all_to_all | solution.py:161
  57.8 0.1 copy.79
  58.0 0.2 slice_convert_fusion.2
  58.2 0.2 copy.81
  58.4 0.3 copy.137
  58.7 0.2 copy.87
  58.8 0.2 copy.82
  59.0 0.2 copy.80
  59.2 0.6 copy_bitcast_fusion
  59.8 1.1 multiply_reduce_fusion.9
  60.9 0.1 copy.113
  61.0 1.0 fusion.40
  62.1 0.1 copy.110
  62.2 1.0 fusion.37
  63.2 8.5 %fusion = f32[16,16,1,64]{3,2,1,0:T(1,128)S(1)} fusion(f32[16,16,64,1]{2,3,1,0:T(1,128)S(1)} %bitcast.193, f32[64,64]{1,0:T(8,128)S(1)} %fusion.60, f32[16,16]{1,0:T(8,128)S(1)} %copy.86, pred[64,64]{1,0:T(8,128)(4,1)S(1)} %fusion.61), kind=kOutput, calls=%fused_computation.1 | convolution fusion | flops 14680064 | bytes 152576 | tf_op jit(solution)/shard_map/cnjk,cnj->cnk/dot_general | solution.py:124
  71.7 14.3 %fusion.1 = f32[16,16,1,64]{3,2,1,0:T(1,128)S(1)} fusion(f32[16,16,64,1]{2,3,1,0:T(1,128)S(1)} %bitcast.192, f32[64,64]{1,0:T(8,128)S(1)} %fusion.60, f32[16,16]{1,0:T(8,128)S(1)} %copy.86, pred[64,64]{1,0:T(8,128)(4,1)S(1)} %fusion.61), kind=kOutput, calls=%fused_computation.2 | convolution fusion | flops 14680064 | bytes 152576 | tf_op jit(solution)/shard_map/cnkj,cnj->cnk/dot_general | solution.py:117
  86.0 1.1 fusion.31
  87.1 2.1 %convolution_add_fusion = f32[16,64,128]{2,1,0:T(8,128)S(1)} fusion(f32[16,64,128]{2,1,0:T(8,128)S(1)} %fusion.31, f32[16,64,128]{2,1,0:T(8,128)S(1)} %bitcast.165, f32[16,128,128]{2,1,0:T(8,128)S(1)} %convolution_multiply_fusion.1), kind=kOutput, calls=%fused_computation.14 | convolution fusion | flops 201457664 | bytes 2621440 | tf_op jit(solution)/shard_map/ckt,cst->cks/dot_general | solution.py:122
  89.3 1.1 fusion.33
  90.4 1.1 convolution_add_fusion.1
  91.4 3.2 %multiply_reduce_fusion.4 = (f32[16]{0:T(128)S(1)}, f32[16]{0:T(128)S(1)}, f32[16]{0:T(128)S(1)}, f32[16,8192]{1,0:T(8,128)S(1)}, f32[16]{0:T(128)S(1)}, /*index...) fusion(f32[16,8192]{1,0:T(8,128)S(1)} %bitcast.168, ...), kind=kLoop, calls=%fused_computation.60 | loop fusion | flops 3407728 | bytes 7864960 | tf_op jit(solution)/shard_map/reduce_sum | solution.py:149
  94.6 0.4 fusion.29
  95.0 0.3 fusion.28
  95.4 0.3 fusion.30
  95.7 0.1 pad_maximum_fusion.1
  95.8 8.2 %copy.88 = bf16[3,16,8192]{1,0,2:T(4,128)(2,1)} copy(bf16[3,16,8192]{2,1,0:T(8,128)(2,1)S(1)} %pad_maximum_fusion.1) | data formatting | bytes 1572864 | tf_op jit(solution)/shard_map/stack | solution.py:153
  104.0 12.9 %reshape.129 = bf16[64,2,3072]{2,1,0:T(2,128)(2,1)S(1)} reshape(bf16[8192,3,16]{2,1,0:T(4,128)(2,1)} %bitcast.155) | data formatting | bytes 1572864
  116.9 30.1 %all_to_all.35 = bf16[64,2,3072]{2,1,0:T(2,128)(2,1)S(1)} all-to-all(bf16[64,2,3072]{2,1,0:T(2,128)(2,1)S(1)} %reshape.129), channel_id=1, replica_groups=mesh['ctx'=64,'tp'=4] {'ctx'}, dimensions={0} | all-to-all | bytes 1572864 | tf_op jit(solution)/shard_map/all_to_all | solution.py:183
  147.1 10.8 %reshape.130 = bf16[8192,3,16]{2,1,0:T(4,128)(2,1)} reshape(bf16[64,2,3072]{2,1,0:T(2,128)(2,1)S(1)} %all_to_all.35) | data formatting | bytes 1572864
  157.8 7.8 %copy.102 = bf16[3,16,64,128]{3,2,1,0:T(8,128)(2,1)S(1)} copy(bf16[3,16,64,128]{1,0,3,2:T(4,128)(2,1)} %bitcast.156) | data formatting | bytes 1572864 | tf_op jit(solution)/shard_map/all_to_all | solution.py:183
  165.8 0.2 copy.90
  165.9 7.3 %convolution_convert_fusion = bf16[128,4096]{1,0:T(8,128)(2,1)} fusion(bf16[1024,128]{1,0:T(8,128)(2,1)S(1)} %bitcast.182, bf16[4096,1024]{1,0:T(8,128)(2,1)} %param.13), kind=kOutput, calls=%fused_computation.3 | convolution fusion | flops 1074266112 | bytes 9699328 | tf_op jit(solution)/shard_map/dot_general | solution.py:204
  173.2 0.1 copy.93
  173.4 0.1 copy.94
  173.5 1.1 fusion.11
  174.5 1.8 convolution_multiply_fusion
  176.4 1.9 fusion.10
  178.4 0.7 reshape.131
  179.1 18.4 %all_to_all.36 = f32[64,1,416]{2,1,0:T(1,128)S(1)} all-to-all(f32[64,1,416]{2,1,0:T(1,128)S(1)} %reshape.131), channel_id=1, replica_groups=mesh['ctx'=64,'tp'=4] {'ctx'}, dimensions={0} | all-to-all | bytes 212992 | tf_op jit(solution)/shard_map/all_to_all | solution.py:198
  197.5 0.5 broadcast.78
  198.0 1.0 reduce
  199.0 0.3 reshape.132
  199.3 0.2 slice.184
  199.5 0.2 slice.185
  199.7 0.8 copy.104
  200.5 0.8 copy.105
  201.3 0.2 copy.106
  201.5 0.7 reshape.120
  202.2 0.2 copy.92
  202.3 0.9 copy.97
  203.2 0.2 copy.91
  203.4 0.9 copy.96
  (29 shorter events, 0.8 us)
Async XLA Ops:
  7.2 22.3 %copy-start = (f32[1024,3,3]{0,2,1:T(4,128)S(1)}, f32[1024,3,3]{0,2,1:T(4,128)}, u32[]{:S(2)}) copy-start(f32[1024,3,3]{0,2,1:T(4,128)} %param.14) | copy-start | bytes 110596
  13.6 44.2 %all-to-all-start = ((bf16[4,1024,128]{2,0,1:T(4,128)(2,1)}), bf16[4,1024,128]{2,0,1:T(4,128)(2,1)S(1)}, u32[]{:S(2)}, u32[]{:S(2)}) async-start(bf16[4,1024,128]{2,0,1:T(4,128)(2,1)} %copy.78), calls=%async_computation | async-start | bytes 2097152 | tf_op jit(solution)/shard_map/all_to_all | solution.py:161
  27.3 176.9 %reduce-scatter.2.cloned.1.call-start = ((), (), s32[]{:S(2)}) async-start(), calls=%async_computation.4 | async-start | bytes 1310720 | tf_op jit(solution)/shard_map/reduce_scatter | solution.py:208
Sparse Core Ops, SparseCore 0:
  173.4 17.3 reduce-scatter.1
where the time goes:
time: 215 us; the launch traced here: 211 us
  local copies, waits for them, and re-layouts  56 us (26%)
  blocking collectives  48.6 us (23%)
  matrix products  44.2 us (21%)
  waiting for transfers between devices  26.2 us (12%)
  between operations  14.6 us (7%)
  starting transfers between devices  13.9 us (6%)
  other arithmetic  7.87 us (4%)
    unnamed x18, local copies, waits for them, and re-layouts  33.2 us
    all_to_all x1, blocking collectives, on_device(): lax.all_to_all(rounded, 'ctx', split_axis=2, concat_axis=1, tiled=True)  30.1 us
    all_to_all x1, waiting for transfers between devices, on_device(): lax.all_to_all(stacked_in, 'ctx', split_axis=1, concat_axis=2, tiled=True)  26.1 us
    all_to_all x1, blocking collectives, on_device(): lax.all_to_all(spread, 'ctx', split_axis=0, concat_axis=0, tiled=True)  18.4 us
    dot_general x1, matrix products, blocked_backward(): carried = jnp.einsum('cnkj,cnj->cnk', carry_mat, ends, precision=highest)  14.3 us
    all_to_all x1, starting transfers between devices, on_device(): lax.all_to_all(stacked_in, 'ctx', split_axis=1, concat_axis=2, tiled=True)  13.7 us
    dot_general x1, matrix products, blocked_backward(): later = jnp.einsum('cnjk,cnj->cnk', carry_mat, starts, precision=highest)  8.51 us
    another operation x1, local copies, waits for them, and re-layouts, blocked_backward(): return (jnp.stack(pre_grads), grad_residues, grad_skip, jnp.stack(tap_cols))  8.24 us
  transfers between devices with their start and end apart: 2, of which 1 were waited for; matrix products, arithmetic and copies ran while one was open for 8% of the time, Pallas kernels for 0%

commit v1 on v0

--- a/solution.py
+++ b/solution.py
@@ -74,25 +74,31 @@
 
 def blocked_backward(pres, cotangent, taps, residue_table, rate_table, skip_table):
     tap_count = taps.shape[-1]
-    chans, length = cotangent.shape
-    block_len = min(128, length)
-    blocks = length // block_len
+    blocks, chans, block_len = cotangent.shape
 
     def delayed(values_in, amount):
-        return jnp.pad(values_in, ((0, 0), (amount, 0)))[:, :length]
+        prev = jnp.pad(values_in[:-1], ((1, 0), (0, 0), (0, 0)))
+        return jnp.concatenate(
+            [prev[:, :, block_len - amount :], values_in[:, :, : block_len - amount]], axis=2
+        )
 
     def advance(values_in, amount):
-        return jnp.pad(values_in, ((0, 0), (0, amount)))[:, amount:]
+        nxt = jnp.pad(values_in[1:], ((0, 1), (0, 0), (0, 0)))
+        return jnp.concatenate([values_in[:, :, amount:], nxt[:, :, :amount]], axis=2)
+
+    def per_chan(column):
+        return column[None, :, None]
 
     feats = []
     for m in range(3):
-        acc = taps[m][:, 0:1] * pres[m]
+        acc = per_chan(taps[m][:, 0]) * pres[m]
         for j in range(1, tap_count):
-            acc = acc + taps[m][:, j : j + 1] * delayed(pres[m], j)
+            acc = acc + per_chan(taps[m][:, j]) * delayed(pres[m], j)
         feats.append(acc)
     query_feat, key_feat, value_feat = feats
-    mixed = key_feat * value_feat
-    grad_conv = cotangent * query_feat
+    xb = key_feat * value_feat
+    gb = cotangent * query_feat
+    skip_b = per_chan(skip_table)
 
     rate = rate_table[:, :, None]
     offs = jnp.arange(block_len, dtype=jnp.float32)
@@ -102,8 +108,6 @@
     toeplitz = (
         jnp.einsum("cns,cnt->cst", residue_table[:, :, None] * down, up, precision=highest) * tri
     )
-    xb = mixed.reshape(chans, blocks, block_len)
-    gb = grad_conv.reshape(chans, blocks, block_len)
 
     idx = jnp.arange(blocks, dtype=jnp.float32)
     gap = idx[:, None] - 1.0 - idx[None, :]
@@ -111,56 +115,69 @@
         gap >= 0, jnp.exp(-rate[..., None] * block_len * jnp.maximum(gap, 0.0)), 0.0
     )
 
-    conv_intra = jnp.einsum("cks,cst->ckt", xb, toeplitz, precision=highest)
+    conv_intra = jnp.einsum("kcs,cst->kct", xb, toeplitz, precision=highest)
     tail_w = jnp.exp(-rate * (block_len - 1 - offs))
-    ends = jnp.einsum("cks,cns->cnk", xb, tail_w, precision=highest)
-    carried = jnp.einsum("cnkj,cnj->cnk", carry_mat, ends, precision=highest)
+    ends = jnp.einsum("kcs,cns->cnk", xb, tail_w, precision=highest)
+    carried = jnp.sum(carry_mat * ends[:, :, None, :], axis=3)
     lead_w = residue_table[:, :, None] * jnp.exp(-rate * (offs + 1.0))
-    conv_carry = jnp.einsum("cnk,cnt->ckt", carried, lead_w, precision=highest)
-    conv_out = (conv_intra + conv_carry).reshape(chans, length)
-
-    back_intra = jnp.einsum("ckt,cst->cks", gb, toeplitz, precision=highest)
-    starts = jnp.einsum("ckt,cnt->cnk", gb, up, precision=highest)
-    later = jnp.einsum("cnjk,cnj->cnk", carry_mat, starts, precision=highest)
+    conv_carry = jnp.einsum("cnk,cnt->kct", carried, lead_w, precision=highest)
+    conv_out = conv_intra + conv_carry
+
+    back_intra = jnp.einsum("kct,cst->kcs", gb, toeplitz, precision=highest)
+    starts = jnp.einsum("kct,cnt->cnk", gb, up, precision=highest)
+    later = jnp.sum(carry_mat * starts[:, :, :, None], axis=2)
     back_w = jnp.exp(-rate * (block_len - offs))
     back_carry = jnp.einsum(
-        "cnk,cns->cks", later, residue_table[:, :, None] * back_w, precision=highest
-    )
-    grad_mixed = (back_intra + back_carry).reshape(chans, length) + skip_table[:, None] * grad_conv
-
-    pairs = jnp.einsum("cks,ckt->cst", xb, gb, precision=highest) * tri
+        "cnk,cns->kcs", later, residue_table[:, :, None] * back_w, precision=highest
+    )
+    grad_mixed = back_intra + back_carry + skip_b * gb
+
+    pairs = jnp.einsum("kcs,kct->cst", xb, gb, precision=highest) * tri
     paired = jnp.einsum("cst,cnt->cns", pairs, up, precision=highest)
     res_intra = jnp.sum(paired * down, axis=2)
-    lead_sums = jnp.einsum("cks,cns->cnk", xb, back_w, precision=highest)
+    lead_sums = jnp.einsum("kcs,cns->cnk", xb, back_w, precision=highest)
     grad_residues = res_intra + jnp.sum(later * lead_sums, axis=2)
-    grad_skip = jnp.sum(grad_conv * mixed, axis=1)
-
-    grad_query = cotangent * (conv_out + skip_table[:, None] * mixed)
+    grad_skip = jnp.sum(gb * xb, axis=(0, 2))
+
+    grad_query = cotangent * (conv_out + skip_b * xb)
     stream_grads = (grad_query, grad_mixed * value_feat, grad_mixed * key_feat)
     pre_grads = []
     tap_cols = []
     for m in range(3):
-        acc = taps[m][:, 0:1] * stream_grads[m]
+        acc = per_chan(taps[m][:, 0]) * stream_grads[m]
         for j in range(1, tap_count):
-            acc = acc + taps[m][:, j : j + 1] * advance(stream_grads[m], j)
+            acc = acc + per_chan(taps[m][:, j]) * advance(stream_grads[m], j)
         pre_grads.append(acc)
         tap_cols.append(
             jnp.stack(
-                [jnp.sum(stream_grads[m] * delayed(pres[m], j), axis=1) for j in range(tap_count)],
+                [jnp.sum(stream_grads[m] * pres[m], axis=(0, 2))]
+                + [
+                    jnp.sum(stream_grads[m] * delayed(pres[m], j), axis=(0, 2))
+                    for j in range(1, tap_count)
+                ],
                 axis=-1,
             )
         )
-    return (jnp.stack(pre_grads), grad_residues, grad_skip, jnp.stack(tap_cols))
+    return (jnp.stack(pre_grads, axis=1), grad_residues, grad_skip, jnp.stack(tap_cols))
 
 
 def on_device(
     query_pre, key_pre, value_pre, grad_out, w_value, short_taps, residues, decay_rates, skip
 ):
     tap_count = short_taps.shape[2]
-    stacked_in = jnp.stack([query_pre.T, key_pre.T, value_pre.T, grad_out.T])
-    gathered_in = lax.all_to_all(stacked_in, "ctx", split_axis=1, concat_axis=2, tiled=True)
-    regrouped = (gathered_in[0], gathered_in[1], gathered_in[2], gathered_in[3])
-    local_chans = regrouped[0].shape[0]
+    owners = lax.axis_size("ctx")
+    tokens_here, chans_here = query_pre.shape
+    local_chans = chans_here // owners
+
+    def to_owner_form(values_in):
+        return jnp.transpose(values_in.reshape(tokens_here, owners, local_chans), (1, 2, 0))
+
+    stacked_in = jnp.stack(
+        [to_owner_form(query_pre), to_owner_form(key_pre), to_owner_form(value_pre), to_owner_form(grad_out)],
+        axis=1,
+    )
+    gathered_in = lax.all_to_all(stacked_in, "ctx", split_axis=0, concat_axis=0, tiled=True)
+    regrouped = tuple(gathered_in[:, i].astype(jnp.float32) for i in range(4))
     begin_at = lax.axis_index("ctx") * local_chans
 
     def own_rows(table):
@@ -168,23 +185,19 @@
 
     taps_here = jnp.transpose(own_rows(short_taps), (1, 0, 2))
     pre_grads, part_residues, part_skip, part_taps = blocked_backward(
-        (
-            regrouped[0].astype(jnp.float32),
-            regrouped[1].astype(jnp.float32),
-            regrouped[2].astype(jnp.float32),
-        ),
-        regrouped[3].astype(jnp.float32),
+        (regrouped[0], regrouped[1], regrouped[2]),
+        regrouped[3],
         taps_here,
         own_rows(residues),
         own_rows(decay_rates),
         own_rows(skip),
     )
     rounded = pre_grads.astype(jnp.bfloat16)
-    returned = lax.all_to_all(rounded, "ctx", split_axis=2, concat_axis=1, tiled=True)
-    query_grad = returned[0].T
-    key_grad = returned[1].T
-    value_grad = returned[2].T
-    owners = lax.axis_size("ctx")
+    returned = lax.all_to_all(rounded, "ctx", split_axis=0, concat_axis=0, tiled=True)
+    flat = jnp.transpose(returned, (1, 3, 0, 2)).reshape(3, tokens_here, chans_here)
+    query_grad = flat[0]
+    key_grad = flat[1]
+    value_grad = flat[2]
     local_rows = part_residues.shape[0]
     packed = jnp.concatenate(
         [

time: 215 us -> 151 us (0.70); the launches traced: 211 us -> 151 us
  local copies, waits for them, and re-layouts: 56 us -> 17.1 us
  matrix products: 44.2 us -> 18.6 us
  other arithmetic: 7.87 us -> 11.9 us
    unnamed x18 -> x17, local copies, waits for them, and re-layouts: 33.2 us -> 9.01 us
    dot_general x10 -> x8, matrix products: 33.1 us -> 10.9 us  [the longest x1 2.78 us: blocked_backward(): back_intra = jnp.einsum('kct,cst->kcs', gb, toeplitz, precision=highest)]
    another operation x2, local copies, waits for them, and re-layouts: 10 us -> 1.83 us  [the longest x1 1.31 us: on_device(): jnp.stack([to_owner_form(query_pre), to_owner_form(key_pre), to_owner_for...]
    all_to_all x2 -> x1, local copies, waits for them, and re-layouts: 7.98 us -> 0.14 us  [on_device(): lax.all_to_all(rounded, 'ctx', split_axis=0, concat_axis=0, tiled=True)]
    reduce_sum x2 -> x3, other arithmetic: 4.27 us -> 8.42 us  [the longest x1 5.84 us: blocked_backward(): carried = jnp.sum(carry_mat * ends[:, :, None, :], axis=3)]
    dot_general x1, matrix products: 7.27 us -> 3.84 us  [on_device(): lax.dot_general(value_grad, w_value, (((1,), (1,)), ((), ())), preferred_...]
    slice x4 -> x26, local copies, waits for them, and re-layouts: 0.58 us -> 3.24 us  [the longest x6 1.22 us: advance(): values_in[:, :, amount:]]
  transfers between devices with their start and end apart: 2 -> 2, of which waited for: 1 -> 1; matrix products, arithmetic and copies ran while one was open for 8% -> 11% of each run, Pallas kernels for 0% -> 0%
where the time goes in v1:
time: 151 us
  blocking collectives  48.5 us (32%)
  waiting for transfers between devices  26.3 us (17%)
  matrix products  18.6 us (12%)
  local copies, waits for them, and re-layouts  17.1 us (11%)
  between operations  14.5 us (10%)
  starting transfers between devices  13.7 us (9%)
  other arithmetic  11.9 us (8%)
    all_to_all x1, blocking collectives, on_device(): lax.all_to_all(rounded, 'ctx', split_axis=0, concat_axis=0, tiled=True)  30.1 us
    all_to_all x1, waiting for transfers between devices, on_device(): lax.all_to_all(stacked_in, 'ctx', split_axis=0, concat_axis=0, tiled=True)  26.3 us
    all_to_all x1, blocking collectives, on_device(): lax.all_to_all(spread, 'ctx', split_axis=0, concat_axis=0, tiled=True)  18.4 us
    all_to_all x1, starting transfers between devices, on_device(): lax.all_to_all(stacked_in, 'ctx', split_axis=0, concat_axis=0, tiled=True)  13.7 us
    unnamed x17, local copies, waits for them, and re-layouts  9.01 us
    reduce_sum x1, other arithmetic, blocked_backward(): carried = jnp.sum(carry_mat * ends[:, :, None, :], axis=3)  5.84 us
    dot_general x1, matrix products, on_device(): lax.dot_general(value_grad, w_value, (((1,), (1,)), ((), ())), preferred_...  3.84 us
  transfers between devices with their start and end apart: 2, of which 1 were waited for; matrix products, arithmetic and copies ran while one was open for 11% of the time, Pallas kernels for 0%

profile of v1, /device:TPU:8, one launch (start us, length us, event | category | flops | bytes accessed | tf_op | source)
XLA Modules:
  0.0 150.7 jit_solution(9347759283955127362)
XLA Ops:
  7.2 1.1 copy.76
  8.3 1.1 copy.77
  9.4 1.1 copy.78
  10.6 1.1 copy.79
  11.7 0.1 pad_maximum_fusion
  11.8 1.3 copy.80
  13.2 13.7 %all-to-all-start = ((bf16[64,4,16,128]{3,2,1,0:T(8,128)(2,1)}), bf16[64,4,16,128]{3,2,1,0:T(8,128)(2,1)S(1)}, u32[]{:S(2)}, u32[]{:S(2)}) async-start(bf16[64,4,16,128]{3,2,1,0:T(8,128)(2,1)} %copy.80), calls=%async_computation | async-start | bytes 2097152 | tf_op jit(solution)/shard_map/all_to_all | solution.py:179
  26.9 0.8 broadcast_multiply_fusion
  27.8 0.8 dynamic_slice.15
  28.8 0.1 dynamic-slice_bitcast_fusion
  28.9 0.1 fusion.50
  29.1 1.9 %convolution_multiply_fusion.1 = f32[16,128,128]{2,1,0:T(8,128)S(1)} fusion(f32[128,128]{1,0:T(8,128)S(1)} %fusion.48, f32[16,16]{1,0:T(8,128)S(1)} %copy.84, f32[16,16]{1,0:T(8,128)S(1)} %copy.83, f32[16,16]{1,0:T(8,128)S(1)} %copy.82), kind=kOutput, calls=%fused_computation.5 | convolution fusion | flops 50692096 | bytes 1117184 | tf_op jit(solution)/shard_map/cns,cnt->cst/dot_general | solution.py:109
  31.0 26.3 %all-to-all-done = bf16[64,4,16,128]{3,2,1,0:T(8,128)(2,1)S(1)} async-done(((bf16[64,4,16,128]{3,2,1,0:T(8,128)(2,1)}), bf16[64,4,16,128]{3,2,1,0:T(8,128)(2,1)S(1)}, u32[]{:S(2)}, u32[]{:S(2)}) %all-to-all-start) | async-done | bytes 1048608 | tf_op jit(solution)/shard_map/all_to_all | solution.py:179
  57.4 0.2 fusion.51
  57.5 0.1 copy_convert_fusion.2
  57.7 0.2 pad_slice_fusion.10
  57.9 0.2 pad_slice_fusion.11
  58.1 0.3 copy_convert_fusion
  58.4 0.2 pad_slice_fusion.4
  58.6 0.2 pad_slice_fusion.5
  58.9 0.2 pad_slice_fusion.8
  59.1 0.2 pad_slice_fusion.9
  59.3 1.5 %multiply_reduce_fusion.11 = (f32[16]{0:T(128)S(1)}, f32[64,16,128]{2,0,1:T(8,128)S(1)}, f32[64,16,128]{2,0,1:T(8,128)S(1)}, f32[64,16,128]{2,0,1:T(8,128)S(1)}, f32[64,16,128]{2,0,1:T(8,128)S(1)}) fusion(f32[64,16,126]{2,0,1:T(8,128)S(1)} %bitcast.148, f32[64,16,2]{2,0,1:T(8,128)S(1)} %pad_slice_fusion.4, f32[16]{0:T(128)S(1)} %get-tuple-element.78, ...), kind=kLoop, calls=%fused_computation.54 | loop fusion | flops 3801072 | bytes 6292096 | tf_op jit(solution)/shard_map/reduce_sum | solution.py:140
  60.8 1.0 fusion.28
  61.8 1.0 fusion.21
  62.8 5.8 %multiply_reduce_fusion.1 = (f32[16,16,64]{2,1,0:T(8,128)S(1)}, f32[16,16,64]{2,1,0:T(8,128)S(1)}) fusion(f32[16,16,64]{2,1,0:T(8,128)S(1)} %fusion.21, f32[64,64]{1,0:T(8,128)S(1)} %fusion.49, f32[16,16]{1,0:T(8,128)S(1)} %copy.87, pred[64,64]{1,0:T(8,128)(4,1)S(1)} %fusion.50, f32[16,16,64]{2,1,0:T(8,128)S(1)} %fusion.28), kind=kLoop, calls=%fused_computation.1 | loop fusion | flops 6258688 | bytes 283648 | tf_op jit(solution)/shard_map/reduce_sum | solution.py:121
  68.6 1.1 fusion.19
  69.8 2.8 %multiply_reduce_fusion.7 = (f32[16]{0:T(128)S(1)}, f32[16]{0:T(128)S(1)}, f32[16]{0:T(128)S(1)}, f32[64,16,128]{2,0,1:T(8,128)S(1)}, f32[16]{0:T(128)S(1)}, /*i...) fusion(bf16[64,1,16,128]{3,2,1,0:T(8,128)(2,1)S(1)} %get-tuple-element.50, ...), kind=kOutput, calls=%fused_computation.50 | convolution fusion | flops 204341152 | bytes 6816192 | tf_op jit(solution)/shard_map/kct,cst->kcs/dot_general | solution.py:126
  72.8 1.1 fusion.24
  74.0 1.1 fusion.4
  75.2 0.2 slice.285
  75.4 0.2 slice.283
  75.6 0.2 slice.292
  75.8 0.2 slice.290
  76.0 0.2 slice.293
  76.2 0.2 slice.295
  76.4 1.1 multiply_reduce_fusion.10
  77.5 0.4 fusion.17
  77.9 0.4 fusion.16
  78.3 0.1 pad_maximum_fusion.1
  78.4 0.5 copy.89
  78.9 30.1 %all_to_all.15 = bf16[64,3,16,128]{3,2,1,0:T(8,128)(2,1)S(1)} all-to-all(bf16[64,3,16,128]{3,2,1,0:T(8,128)(2,1)S(1)} %copy.89), channel_id=1, replica_groups=mesh['ctx'=64,'tp'=4] {'ctx'}, dimensions={0} | all-to-all | bytes 1572864 | tf_op jit(solution)/shard_map/all_to_all | solution.py:196
  109.0 0.1 copy.135
  109.2 0.1 fusion.52
  109.3 3.8 %convolution_convert_fusion = bf16[128,4096]{1,0:T(8,128)(2,1)} fusion(bf16[128,1024]{0,1:T(8,128)(2,1)S(1)} %bitcast.166, bf16[4096,1024]{1,0:T(8,128)(2,1)S(1)} %bitcast.161), kind=kOutput, calls=%fused_computation.3 | convolution fusion | flops 1074266112 | bytes 9699328 | tf_op jit(solution)/shard_map/dot_general | solution.py:217
  113.2 0.1 copy.91
  113.4 0.1 copy.92
  113.4 1.1 fusion.6
  114.5 1.8 %convolution_multiply_fusion = f32[16,128,128]{2,1,0:T(8,128)S(1)} fusion(f32[64,16,128]{2,0,1:T(8,128)S(1)} %get-tuple-element.43, f32[64,16,128]{2,0,1:T(8,128)S(1)} %get-tuple-element.42, f32[128,128]{1,0:T(8,128)S(1)} %fusion.48), kind=kOutput, calls=%fused_computation.4 | convolution fusion | flops 201588736 | bytes 2162688 | tf_op jit(solution)/shard_map/kcs,kct->cst/dot_general | solution.py:135
  116.3 1.9 %fusion.5 = f32[16,16]{1,0:T(8,128)S(1)} fusion(f32[16,128,128]{2,1,0:T(8,128)S(1)} %convolution_multiply_fusion, f32[16,16]{1,0:T(8,128)S(1)} %copy.84, f32[16,16]{1,0:T(8,128)S(1)} %copy.83), kind=kOutput, calls=%fused_computation.15 | convolution fusion | flops 50462464 | bytes 1051648 | tf_op jit(solution)/shard_map/cst,cnt->cns/dot_general | solution.py:136
  118.2 0.1 pad_maximum_fusion.8
  118.3 0.7 reshape.126
  119.0 18.4 %all_to_all.16 = f32[64,1,416]{2,1,0:T(1,128)S(1)} all-to-all(f32[64,1,416]{2,1,0:T(1,128)S(1)} %reshape.126), channel_id=1, replica_groups=mesh['ctx'=64,'tp'=4] {'ctx'}, dimensions={0} | all-to-all | bytes 212992 | tf_op jit(solution)/shard_map/all_to_all | solution.py:211
  137.5 0.5 broadcast.68
  138.0 1.0 reduce
  138.9 0.3 reshape.127
  139.3 0.2 slice.300
  139.5 0.2 slice.301
  139.7 0.8 copy.101
  140.5 0.8 copy.102
  141.3 0.2 copy.103
  141.5 0.7 reshape.124
  142.1 0.8 copy.95
  143.0 0.8 copy.94
  (43 shorter events, 1.1 us)
Async XLA Ops:
  7.2 21.6 %copy-start = (f32[1024,3,3]{0,2,1:T(4,128)S(1)}, f32[1024,3,3]{0,2,1:T(4,128)}, u32[]{:S(2)}) copy-start(f32[1024,3,3]{0,2,1:T(4,128)} %param.14) | copy-start | bytes 110596
  13.2 44.2 %all-to-all-start = ((bf16[64,4,16,128]{3,2,1,0:T(8,128)(2,1)}), bf16[64,4,16,128]{3,2,1,0:T(8,128)(2,1)S(1)}, u32[]{:S(2)}, u32[]{:S(2)}) async-start(bf16[64,4,16,128]{3,2,1,0:T(8,128)(2,1)} %copy.80), calls=%async_computation | async-start | bytes 2097152 | tf_op jit(solution)/shard_map/all_to_all | solution.py:179
  26.8 117.0 %reduce-scatter.2.cloned.1.call-start = ((), (), s32[]{:S(2)}) async-start(), calls=%async_computation.4 | async-start | bytes 1310720 | tf_op jit(solution)/shard_map/reduce_scatter | solution.py:221
  76.4 32.9 %slice-start = ((s8[8388608]{0:T(1024)(128)(4,1)}), s8[4194304]{0:T(1024)(128)(4,1)S(1)}, s32[]{:S(2)}) async-start(s8[8388608]{0:T(1024)(128)(4,1)} %bitcast.160), calls=%async_computation.5 | async-start | bytes 8388608
  77.9 31.4 %slice-start.1 = ((s8[8388608]{0:T(1024)(128)(4,1)}), s8[4194304]{0:T(1024)(128)(4,1)S(1)}, s32[]{:S(2)}) async-start(s8[8388608]{0:T(1024)(128)(4,1)} %bitcast.160), calls=%async_computation.6 | async-start | bytes 8388608
Sparse Core Ops, SparseCore 0:
  113.3 17.4 reduce-scatter.1

commit v2 on v1

--- a/solution.py
+++ b/solution.py
@@ -192,13 +192,8 @@
         own_rows(decay_rates),
         own_rows(skip),
     )
-    rounded = pre_grads.astype(jnp.bfloat16)
-    returned = lax.all_to_all(rounded, "ctx", split_axis=0, concat_axis=0, tiled=True)
-    flat = jnp.transpose(returned, (1, 3, 0, 2)).reshape(3, tokens_here, chans_here)
-    query_grad = flat[0]
-    key_grad = flat[1]
-    value_grad = flat[2]
     local_rows = part_residues.shape[0]
+    mode_count = part_residues.shape[1]
     packed = jnp.concatenate(
         [
             part_residues,
@@ -207,10 +202,32 @@
         ],
         axis=1,
     )
-    spread = jnp.broadcast_to(packed[None], (owners,) + packed.shape)
-    everyone = lax.all_to_all(spread, "ctx", split_axis=0, concat_axis=0, tiled=True)
-    everyone = everyone.reshape(owners * local_rows, packed.shape[1])
-    mode_count = part_residues.shape[1]
+    packed_hi = packed.astype(jnp.bfloat16)
+    packed_lo = (packed - packed_hi.astype(jnp.float32)).astype(jnp.bfloat16)
+    split_pair = jnp.concatenate([packed_hi, packed_lo], axis=1).reshape(-1)
+    lane_len = pre_grads.shape[-1]
+    side_rows = -(-split_pair.shape[0] // lane_len)
+    side_rows = -(-side_rows // 8) * 8
+    side = jnp.pad(split_pair, (0, side_rows * lane_len - split_pair.shape[0])).reshape(side_rows, lane_len)
+    rounded = pre_grads.astype(jnp.bfloat16)
+    grad_rows = rounded.shape[1] * rounded.shape[2]
+    payload = jnp.concatenate(
+        [
+            rounded.reshape(owners, grad_rows, lane_len),
+            jnp.broadcast_to(side[None], (owners, side_rows, lane_len)),
+        ],
+        axis=1,
+    )
+    returned = lax.all_to_all(payload, "ctx", split_axis=0, concat_axis=0, tiled=True)
+    grads_back = returned[:, :grad_rows].reshape(rounded.shape)
+    flat = jnp.transpose(grads_back, (1, 3, 0, 2)).reshape(3, tokens_here, chans_here)
+    query_grad = flat[0]
+    key_grad = flat[1]
+    value_grad = flat[2]
+    width = packed.shape[1]
+    side_back = returned[:, grad_rows:].reshape(owners, -1)[:, : split_pair.shape[0]]
+    side_back = side_back.reshape(owners * local_rows, 2 * width).astype(jnp.float32)
+    everyone = side_back[:, :width] + side_back[:, width:]
     d_residues = everyone[:, :mode_count]
     d_skip = everyone[:, mode_count]
     d_taps = everyone[:, mode_count + 1 :].reshape(-1, part_taps.shape[0], tap_count)

time: 151 us -> 168 us (1.11); the launches traced: 151 us -> 165 us
  blocking collectives: 48.5 us -> 32.7 us
  local copies, waits for them, and re-layouts: 17.1 us -> 25.8 us
  other arithmetic: 11.9 us -> 19.5 us
  waiting for transfers between devices: 26.3 us -> 33.8 us
  matrix products: 18.6 us -> 24.8 us
    all_to_all x2 -> x1, blocking collectives: 48.5 us -> 32.7 us  [on_device(): lax.all_to_all(payload, 'ctx', split_axis=0, concat_axis=0, tiled=True)]
    reduce_scatter x1, waiting for transfers between devices: 0.01 us -> 11.9 us  [on_device(): lax.psum_scatter(narrowed.astype(jnp.float32).astype(jnp.bfloat16), 'tp',...]
    slice x6, local copies, waits for them, and re-layouts: 0.24 us -> 5.04 us  [advance(): nxt[:, :, :amount]]
    all_to_all x1, waiting for transfers between devices: 26.3 us -> 21.9 us  [on_device(): lax.all_to_all(stacked_in, 'ctx', split_axis=0, concat_axis=0, tiled=True)]
    dot_general x1, matrix products: 3.84 us -> 7.27 us  [on_device(): lax.dot_general(value_grad, w_value, (((1,), (1,)), ((), ())), preferred_...]
    slice x6, local copies, waits for them, and re-layouts: 1.22 us -> 4.43 us  [advance(): values_in[:, :, amount:]]
    reduce_sum x1, other arithmetic: 1.06 us -> 3.58 us  [blocked_backward(): jnp.sum(stream_grads[m] * pres[m], axis=(0, 2))]
    unnamed x17 -> x70, local copies, waits for them, and re-layouts: 9.01 us -> 7.16 us
  transfers between devices with their start and end apart: 2 -> 2, of which waited for: 1 -> 2; matrix products, arithmetic and copies ran while one was open for 11% -> 8% of each run, Pallas kernels for 0% -> 0%
where the time goes in v2:
time: 168 us; the launch traced here: 165 us
  waiting for transfers between devices  33.8 us (20%)
  blocking collectives  32.7 us (19%)
  local copies, waits for them, and re-layouts  25.8 us (15%)
  matrix products  24.8 us (15%)
  other arithmetic  19.5 us (12%)
  between operations  14.7 us (9%)
  starting transfers between devices  13.7 us (8%)
    all_to_all x1, blocking collectives, on_device(): lax.all_to_all(payload, 'ctx', split_axis=0, concat_axis=0, tiled=True)  32.7 us
    all_to_all x1, waiting for transfers between devices, on_device(): lax.all_to_all(stacked_in, 'ctx', split_axis=0, concat_axis=0, tiled=True)  21.9 us
    all_to_all x1, starting transfers between devices, on_device(): lax.all_to_all(stacked_in, 'ctx', split_axis=0, concat_axis=0, tiled=True)  13.7 us
    reduce_scatter x1, waiting for transfers between devices, on_device(): lax.psum_scatter(narrowed.astype(jnp.float32).astype(jnp.bfloat16), 'tp',...  11.9 us
    dot_general x1, matrix products, on_device(): lax.dot_general(value_grad, w_value, (((1,), (1,)), ((), ())), preferred_...  7.27 us
    unnamed x70, local copies, waits for them, and re-layouts  7.16 us
    reduce_sum x1, other arithmetic, blocked_backward(): carried = jnp.sum(carry_mat * ends[:, :, None, :], axis=3)  5.81 us
    slice x6, local copies, waits for them, and re-layouts, advance(): nxt[:, :, :amount]  5.04 us
  transfers between devices with their start and end apart: 2, of which 2 were waited for; matrix products, arithmetic and copies ran while one was open for 8% of the time, Pallas kernels for 0%

profile of v2, /device:TPU:8, one launch (start us, length us, event | category | flops | bytes accessed | tf_op | source)
XLA Modules:
  0.0 165.0 jit_solution(14956382139466685920)
XLA Ops:
  7.2 1.1 copy.80
  8.3 1.1 copy.81
  9.4 1.1 copy.82
  10.6 1.1 copy.83
  11.8 1.3 copy.84
  13.2 13.7 %all-to-all-start = ((bf16[64,4,16,128]{3,2,1,0:T(8,128)(2,1)}), bf16[64,4,16,128]{3,2,1,0:T(8,128)(2,1)S(1)}, u32[]{:S(2)}, u32[]{:S(2)}) async-start(bf16[64,4,16,128]{3,2,1,0:T(8,128)(2,1)} %copy.84), calls=%async_computation | async-start | bytes 2097152 | tf_op jit(solution)/shard_map/all_to_all | solution.py:179
  26.9 0.8 broadcast_multiply_fusion
  27.8 1.4 dynamic_slice.15
  29.3 0.5 iota_subtract_fusion.1
  29.8 0.5 iota_add_fusion.1
  30.4 0.5 iota_subtract_fusion.2
  31.0 0.5 slice_bitcast_fusion.14
  31.5 0.6 slice_bitcast_fusion.10
  32.1 0.7 fusion.50
  32.8 0.7 fusion.49
  33.5 1.9 %convolution_multiply_fusion.1 = f32[16,128,128]{2,1,0:T(8,128)S(1)} fusion(f32[128,128]{1,0:T(8,128)S(1)} %fusion.48, f32[16,16]{1,0:T(8,128)S(1)} %copy.88, f32[16,16]{1,0:T(8,128)S(1)} %copy.87, f32[16,16]{1,0:T(8,128)S(1)} %copy.86), kind=kOutput, calls=%fused_computation.5 | convolution fusion | flops 50692096 | bytes 1117184 | tf_op jit(solution)/shard_map/cns,cnt->cst/dot_general | solution.py:109
  35.5 21.9 %all-to-all-done = bf16[64,4,16,128]{3,2,1,0:T(8,128)(2,1)S(1)} async-done(((bf16[64,4,16,128]{3,2,1,0:T(8,128)(2,1)}), bf16[64,4,16,128]{3,2,1,0:T(8,128)(2,1)S(1)}, u32[]{:S(2)}, u32[]{:S(2)}) %all-to-all-start) | async-done | bytes 1048608 | tf_op jit(solution)/shard_map/all_to_all | solution.py:179
  57.7 0.2 pad_slice_fusion.10
  57.9 0.2 pad_slice_fusion.11
  58.1 0.2 copy_convert_fusion
  58.5 0.2 pad_slice_fusion.4
  58.7 0.2 pad_slice_fusion.5
  58.9 0.2 pad_slice_fusion.8
  59.1 0.2 pad_slice_fusion.9
  59.4 2.1 %multiply_reduce_fusion.11 = (f32[16]{0:T(128)}, f32[64,16,128]{2,0,1:T(8,128)S(1)}, f32[64,16,128]{2,0,1:T(8,128)S(1)}, f32[64,16,128]{2,0,1:T(8,128)S(1)}, f32[64,16,128]{2,0,1:T(8,128)S(1)}) fusion(f32[64,16,126]{2,0,1:T(8,128)S(1)} %bitcast.153, f32[64,16,2]{2,0,1:T(8,128)S(1)} %pad_slice_fusion.4, f32[16]{0:T(128)S(1)} %copy-done.22, ...), kind=kLoop, calls=%fused_computation.56 | loop fusion | flops 3801072 | bytes 6292096 | tf_op jit(solution)/shard_map/reduce_sum | solution.py:140
  61.5 1.0 fusion.28
  62.5 1.0 fusion.21
  63.5 5.8 %multiply_reduce_fusion.1 = (f32[16,16,64]{2,1,0:T(8,128)S(1)}, f32[16,16,64]{2,1,0:T(8,128)S(1)}) fusion(f32[16,16,64]{2,1,0:T(8,128)S(1)} %fusion.21, f32[64,64]{1,0:T(8,128)S(1)} %copy-done.6, f32[16,16]{1,0:T(8,128)S(1)} %copy.91, pred[64,64]{1,0:T(8,128)(4,1)S(1)} %copy-done.7, f32[16,16,64]{2,1,0:T(8,128)S(1)} %fusion.28), kind=kLoop, calls=%fused_computation.1 | loop fusion | flops 6258688 | bytes 283648 | tf_op jit(solution)/shard_map/reduce_sum | solution.py:121
  69.4 1.1 fusion.6
  70.4 1.1 fusion.19
  71.6 2.8 %convolution_multiply_fusion = f32[16,128,128]{2,1,0:T(8,128)} fusion(f32[64,16,128]{2,0,1:T(8,128)S(1)} %get-tuple-element.43, f32[64,16,128]{2,0,1:T(8,128)S(1)} %get-tuple-element.42, f32[128,128]{1,0:T(8,128)S(1)} %fusion.48), kind=kOutput, calls=%fused_computation.4 | convolution fusion | flops 201588736 | bytes 2162688 | tf_op jit(solution)/shard_map/kcs,kct->cst/dot_general | solution.py:135
  74.4 3.3 %multiply_reduce_fusion.7 = (f32[16]{0:T(128)S(1)}, f32[16]{0:T(128)S(1)}, f32[16]{0:T(128)}, f32[64,16,128]{2,0,1:T(8,128)S(1)}, f32[16]{0:T(128)S(1)}, /*index...) fusion(bf16[64,1,16,128]{3,2,1,0:T(8,128)(2,1)S(1)} %get-tuple-element.50, f32[64,16,126]{2,0,1:T(8,128)S(1)} %bitcast.159, ...), kind=kOutput, calls=%fused_computation.52 | convolution fusion | flops 204341152 | bytes 6816192 | tf_op jit(solution)/shard_map/kct,cst->kcs/dot_general | solution.py:126
  77.7 0.8 pad_slice_fusion
  78.6 0.9 pad_slice_fusion.1
  79.5 0.8 pad_slice_fusion.2
  80.3 0.8 pad_slice_fusion.3
  81.2 1.1 fusion.24
  82.3 1.1 fusion.4
  83.5 0.8 pad_slice_fusion.6
  84.3 0.8 pad_slice_fusion.7
  85.2 1.0 slice.305
  86.2 1.0 slice.303
  87.3 3.1 %fusion.5 = f32[16,16]{1,0:T(8,128)S(1)} fusion(f32[16,128,128]{2,1,0:T(8,128)} %convolution_multiply_fusion, f32[16,16]{1,0:T(8,128)S(1)} %copy.88, f32[16,16]{1,0:T(8,128)S(1)} %copy.87), kind=kOutput, calls=%fused_computation.15 | convolution fusion | flops 50462464 | bytes 1051648 | tf_op jit(solution)/shard_map/cst,cnt->cns/dot_general | solution.py:136
  90.3 0.7 maximum_bitcast_fusion.2
  91.1 3.6 %multiply_reduce_fusion.10 = (f32[16]{0:T(128)S(1)}, f32[16]{0:T(128)S(1)}, f32[16]{0:T(128)S(1)}, bf16[64,1,16,128]{3,0,2,1:T(8,128)(2,1)}) fusion(f32[64,16,128]{2,0,1:T(8,128)S(1)} %fusion.4, bf16[64,1,16,128]{3,2,1,0:T(8,128)(2,1)S(1)} %get-tuple-element.53, f32[64,16,126]{2,0,1:T(8,128)S(1)} %bitcast.155, f32[64,16,2]{2,0,1:T(8,128)} %copy-done.1, ...), kind=kLoop, calls=%fused_computation.55 | loop fusion | flops 2228176 | bytes 3146112 | tf_op jit(solution)/shard_map/reduce_sum | solution.py:153
  94.9 1.0 slice.312
  95.9 1.0 slice.310
  96.9 0.2 slice.313
  97.1 0.2 slice.315
  97.6 2.1 %fusion.17 = bf16[64,1,16,128]{3,0,2,1:T(8,128)(2,1)S(1)} fusion(f32[64,16,2]{2,0,1:T(8,128)} %pad_slice_fusion.2, f32[64,16,126]{2,0,1:T(8,128)} %slice.312, f32[16]{0:T(128)S(1)} %copy-done.17, f32[64,16,1]{2,0,1:T(8,128)} %pad_slice_fusion.3, f32[64,16,127]{2,0,1:T(8,128)} %slice.310, f32[16]{0:T(128)S(1)} %copy-done.15, ...), kind=kLoop, calls=%fused_computation.76 | loop fusion | flops 1048576 | bytes 1835200 | tf_op jit(solution)/shard_map/stack | solution.py:161
  99.7 0.4 fusion.16
  100.2 0.5 copy.95
  100.9 32.7 %all_to_all.10 = bf16[64,56,128]{2,1,0:T(8,128)(2,1)S(1)} all-to-all(bf16[64,56,128]{2,1,0:T(8,128)(2,1)S(1)} %pad_maximum_fusion.1), channel_id=1, replica_groups=mesh['ctx'=64,'tp'=4] {'ctx'}, dimensions={0} | all-to-all | bytes 1835008 | tf_op jit(solution)/shard_map/all_to_all | solution.py:221
  133.8 7.3 %convolution_convert_fusion = bf16[128,4096]{1,0:T(8,128)(2,1)} fusion(bf16[128,1024]{0,1:T(8,128)(2,1)S(1)} %bitcast.168, bf16[4096,1024]{1,0:T(8,128)(2,1)} %param.13), kind=kOutput, calls=%fused_computation.3 | convolution fusion | flops 1074266112 | bytes 9699328 | tf_op jit(solution)/shard_map/dot_general | solution.py:234
  141.1 0.9 copy.98
  142.0 0.8 copy.97
  142.8 0.4 reshape.140
  143.2 0.2 slice_add_fusion
  143.5 0.2 slice.326
  143.7 0.8 copy.99
  144.5 0.2 copy.96
  144.6 0.7 reshape.138
  145.3 1.0 slice_reduce_fusion
  146.3 11.9 %reduce-scatter.2.cloned.1.call-done = bf16[32,4096]{1,0:T(8,128)(2,1)} async-done(((bf16[128,4096]{1,0:T(8,128)(2,1)}), bf16[32,4096]{1,0:T(8,128)(2,1)}) %reduce-scatter.2.cloned.1.call-update) | async-done | bytes 262160 | tf_op jit(solution)/shard_map/reduce_scatter | solution.py:238
  (102 shorter events, 2.2 us)
Async XLA Ops:
  7.2 23.7 %copy-start = (f32[1024,3,3]{0,2,1:T(4,128)S(1)}, f32[1024,3,3]{0,2,1:T(4,128)}, u32[]{:S(2)}) copy-start(f32[1024,3,3]{0,2,1:T(4,128)} %param.14) | copy-start | bytes 110596
  13.2 44.2 %all-to-all-start = ((bf16[64,4,16,128]{3,2,1,0:T(8,128)(2,1)}), bf16[64,4,16,128]{3,2,1,0:T(8,128)(2,1)S(1)}, u32[]{:S(2)}, u32[]{:S(2)}) async-start(bf16[64,4,16,128]{3,2,1,0:T(8,128)(2,1)} %copy.84), calls=%async_computation | async-start | bytes 2097152 | tf_op jit(solution)/shard_map/all_to_all | solution.py:179
  26.8 131.4 %reduce-scatter.2.cloned.1.call-start = ((), (), s32[]{:S(2)}) async-start(), calls=%async_computation.3 | async-start | bytes 1310720 | tf_op jit(solution)/shard_map/reduce_scatter | solution.py:238
  57.3 2.0 %copy-start.8 = (f32[16]{0:T(128)S(1)}, f32[16]{0:T(128)}, u32[]{:S(2)}) copy-start(f32[16]{0:T(128)} %get-tuple-element.74) | copy-start | bytes 196
  57.3 2.0 %copy-start.10 = (f32[16]{0:T(128)S(1)}, f32[16]{0:T(128)}, u32[]{:S(2)}) copy-start(f32[16]{0:T(128)} %get-tuple-element.75) | copy-start | bytes 196
  57.4 2.0 %copy-start.12 = (f32[16]{0:T(128)S(1)}, f32[16]{0:T(128)}, u32[]{:S(2)}) copy-start(f32[16]{0:T(128)} %get-tuple-element.76) | copy-start | bytes 196
  57.4 2.0 %copy-start.14 = (f32[16]{0:T(128)S(1)}, f32[16]{0:T(128)}, u32[]{:S(2)}) copy-start(f32[16]{0:T(128)} %get-tuple-element.83) | copy-start | bytes 196
  57.4 2.0 %copy-start.16 = (f32[16]{0:T(128)S(1)}, f32[16]{0:T(128)}, u32[]{:S(2)}) copy-start(f32[16]{0:T(128)} %get-tuple-element.84) | copy-start | bytes 196
  57.4 2.0 %copy-start.18 = (f32[16]{0:T(128)S(1)}, f32[16]{0:T(128)}, u32[]{:S(2)}) copy-start(f32[16]{0:T(128)} %get-tuple-element.85) | copy-start | bytes 196
  57.4 2.0 %copy-start.20 = (f32[16]{0:T(128)S(1)}, f32[16]{0:T(128)}, u32[]{:S(2)}) copy-start(f32[16]{0:T(128)} %get-tuple-element.77) | copy-start | bytes 196
  57.4 2.0 %copy-start.22 = (f32[16]{0:T(128)S(1)}, f32[16]{0:T(128)}, u32[]{:S(2)}) copy-start(f32[16]{0:T(128)} %get-tuple-element.78) | copy-start | bytes 196
  57.4 2.0 %copy-start.24 = (f32[16]{0:T(128)S(1)}, f32[16]{0:T(128)}, u32[]{:S(2)}) copy-start(f32[16]{0:T(128)} %get-tuple-element.79) | copy-start | bytes 196
  58.4 4.2 %copy-start.30 = (f32[128]{0:T(128)S(1)}, f32[128]{0:T(128)}, u32[]{:S(2)}) copy-start(f32[128]{0:T(128)} %iota_subtract_fusion.2) | copy-start | bytes 1540
  58.4 5.1 %copy-start.6 = (f32[64,64]{1,0:T(8,128)S(1)}, f32[64,64]{1,0:T(8,128)}, u32[]{:S(2)}) copy-start(f32[64,64]{1,0:T(8,128)} %fusion.49) | copy-start | bytes 49156
  58.4 5.1 %copy-start.7 = (pred[64,64]{1,0:T(8,128)(4,1)S(1)}, pred[64,64]{1,0:T(8,128)(4,1)}, u32[]{:S(2)}) copy-start(pred[64,64]{1,0:T(8,128)(4,1)} %fusion.50) | copy-start | bytes 12292
  58.7 10.7 %copy-start.1 = (f32[64,16,2]{2,0,1:T(8,128)}, f32[64,16,2]{2,0,1:T(8,128)S(1)}, u32[]{:S(2)}) copy-start(f32[64,16,2]{2,0,1:T(8,128)S(1)} %pad_slice_fusion.4) | copy-start | bytes 24580
  58.7 10.7 %copy-start.27 = (f32[128]{0:T(128)S(1)}, f32[128]{0:T(128)}, u32[]{:S(2)}) copy-start(f32[128]{0:T(128)} %iota_subtract_fusion.1) | copy-start | bytes 1540
  58.9 12.7 %copy-start.2 = (f32[64,16,1]{2,0,1:T(8,128)}, f32[64,16,1]{2,0,1:T(8,128)S(1)}, u32[]{:S(2)}) copy-start(f32[64,16,1]{2,0,1:T(8,128)S(1)} %pad_slice_fusion.5) | copy-start | bytes 12292
  59.3 15.1 %copy-start.26 = (f32[16]{0:T(128)S(1)}, f32[16]{0:T(128)}, u32[]{:S(2)}) copy-start(f32[16]{0:T(128)} %dynamic_slice.15) | copy-start | bytes 196
  71.6 9.6 %copy-start.29 = (f32[128]{0:T(128)S(1)}, f32[128]{0:T(128)}, u32[]{:S(2)}) copy-start(f32[128]{0:T(128)} %iota_add_fusion.1) | copy-start | bytes 1540
  77.7 9.5 %copy-start.28 = (f32[16]{0:T(128)S(1)}, f32[16]{0:T(128)}, u32[]{:S(2)}) copy-start(f32[16]{0:T(128)} %get-tuple-element.41) | copy-start | bytes 196
  77.7 13.3 %copy-start.21 = (f32[16]{0:T(128)S(1)}, f32[16]{0:T(128)}, u32[]{:S(2)}) copy-start(f32[16]{0:T(128)} %get-tuple-element.77) | copy-start | bytes 196
  77.7 13.3 %copy-start.23 = (f32[16]{0:T(128)S(1)}, f32[16]{0:T(128)}, u32[]{:S(2)}) copy-start(f32[16]{0:T(128)} %get-tuple-element.78) | copy-start | bytes 196
  77.7 13.4 %copy-start.25 = (f32[16]{0:T(128)S(1)}, f32[16]{0:T(128)}, u32[]{:S(2)}) copy-start(f32[16]{0:T(128)} %get-tuple-element.79) | copy-start | bytes 196
  83.4 14.1 %copy-start.15 = (f32[16]{0:T(128)S(1)}, f32[16]{0:T(128)}, u32[]{:S(2)}) copy-start(f32[16]{0:T(128)} %get-tuple-element.83) | copy-start | bytes 196
  83.4 14.1 %copy-start.17 = (f32[16]{0:T(128)S(1)}, f32[16]{0:T(128)}, u32[]{:S(2)}) copy-start(f32[16]{0:T(128)} %get-tuple-element.84) | copy-start | bytes 196
  83.4 14.1 %copy-start.19 = (f32[16]{0:T(128)S(1)}, f32[16]{0:T(128)}, u32[]{:S(2)}) copy-start(f32[16]{0:T(128)} %get-tuple-element.85) | copy-start | bytes 196
  84.3 15.4 %copy-start.3 = (f32[64,16,2]{2,0,1:T(8,128)S(1)}, f32[64,16,2]{2,0,1:T(8,128)}, u32[]{:S(2)}) copy-start(f32[64,16,2]{2,0,1:T(8,128)} %pad_slice_fusion) | copy-start | bytes 24580
  84.3 15.4 %copy-start.9 = (f32[16]{0:T(128)S(1)}, f32[16]{0:T(128)}, u32[]{:S(2)}) copy-start(f32[16]{0:T(128)} %get-tuple-element.74) | copy-start | bytes 196
  84.3 15.4 %copy-start.11 = (f32[16]{0:T(128)S(1)}, f32[16]{0:T(128)}, u32[]{:S(2)}) copy-start(f32[16]{0:T(128)} %get-tuple-element.75) | copy-start | bytes 196
  84.3 15.4 %copy-start.13 = (f32[16]{0:T(128)S(1)}, f32[16]{0:T(128)}, u32[]{:S(2)}) copy-start(f32[16]{0:T(128)} %get-tuple-element.76) | copy-start | bytes 196
  85.2 14.6 %copy-start.4 = (f32[64,16,1]{2,0,1:T(8,128)S(1)}, f32[64,16,1]{2,0,1:T(8,128)}, u32[]{:S(2)}) copy-start(f32[64,16,1]{2,0,1:T(8,128)} %pad_slice_fusion.1) | copy-start | bytes 12292
  94.6 5.5 %copy-start.5 = (bf16[64,1,16,128]{3,0,2,1:T(8,128)(2,1)S(1)}, bf16[64,1,16,128]{3,0,2,1:T(8,128)(2,1)}, u32[]{:S(2)}) copy-start(bf16[64,1,16,128]{3,0,2,1:T(8,128)(2,1)} %get-tuple-element.57) | copy-start | bytes 786436
Sparse Core Ops, SparseCore 0:
  141.2 16.9 reduce-scatter.1

commit v3 on v1

--- a/solution.py
+++ b/solution.py
@@ -161,11 +161,21 @@
     return (jnp.stack(pre_grads, axis=1), grad_residues, grad_skip, jnp.stack(tap_cols))
 
 
+def ctx_exchange(values_in):
+    hi = lax.axis_size("ctx_hi")
+    lo = lax.axis_size("ctx_lo")
+    rest = values_in.shape[1:]
+    staged = values_in.reshape((hi, lo) + rest)
+    staged = lax.all_to_all(staged, "ctx_lo", split_axis=1, concat_axis=1, tiled=True)
+    staged = lax.all_to_all(staged, "ctx_hi", split_axis=0, concat_axis=0, tiled=True)
+    return staged.reshape((hi * lo,) + rest)
+
+
 def on_device(
     query_pre, key_pre, value_pre, grad_out, w_value, short_taps, residues, decay_rates, skip
 ):
     tap_count = short_taps.shape[2]
-    owners = lax.axis_size("ctx")
+    owners = lax.axis_size("ctx_hi") * lax.axis_size("ctx_lo")
     tokens_here, chans_here = query_pre.shape
     local_chans = chans_here // owners
 
@@ -176,9 +186,11 @@
         [to_owner_form(query_pre), to_owner_form(key_pre), to_owner_form(value_pre), to_owner_form(grad_out)],
         axis=1,
     )
-    gathered_in = lax.all_to_all(stacked_in, "ctx", split_axis=0, concat_axis=0, tiled=True)
+    gathered_in = ctx_exchange(stacked_in)
     regrouped = tuple(gathered_in[:, i].astype(jnp.float32) for i in range(4))
-    begin_at = lax.axis_index("ctx") * local_chans
+    begin_at = (
+        lax.axis_index("ctx_hi") * lax.axis_size("ctx_lo") + lax.axis_index("ctx_lo")
+    ) * local_chans
 
     def own_rows(table):
         return lax.dynamic_slice_in_dim(table, begin_at, local_chans, 0)
@@ -193,7 +205,7 @@
         own_rows(skip),
     )
     rounded = pre_grads.astype(jnp.bfloat16)
-    returned = lax.all_to_all(rounded, "ctx", split_axis=0, concat_axis=0, tiled=True)
+    returned = ctx_exchange(rounded)
     flat = jnp.transpose(returned, (1, 3, 0, 2)).reshape(3, tokens_here, chans_here)
     query_grad = flat[0]
     key_grad = flat[1]
@@ -208,7 +220,7 @@
         axis=1,
     )
     spread = jnp.broadcast_to(packed[None], (owners,) + packed.shape)
-    everyone = lax.all_to_all(spread, "ctx", split_axis=0, concat_axis=0, tiled=True)
+    everyone = ctx_exchange(spread)
     everyone = everyone.reshape(owners * local_rows, packed.shape[1])
     mode_count = part_residues.shape[1]
     d_residues = everyone[:, :mode_count]
@@ -225,11 +237,18 @@
 
 
 def solution(mesh):
+    ctx_size = mesh.shape["ctx"]
+    lo_size = 8 if ctx_size % 8 == 0 else 1
+    split_mesh = jax.sharding.Mesh(
+        mesh.devices.reshape(ctx_size // lo_size, lo_size, mesh.shape["tp"]),
+        ("ctx_hi", "ctx_lo", "tp"),
+    )
+    ctx = ("ctx_hi", "ctx_lo")
     in_specs = (
-        P("ctx", "tp"),
-        P("ctx", "tp"),
-        P("ctx", "tp"),
-        P("ctx", "tp"),
+        P(ctx, "tp"),
+        P(ctx, "tp"),
+        P(ctx, "tp"),
+        P(ctx, "tp"),
         P(None, "tp"),
         P("tp", None, None),
         P("tp", None),
@@ -237,13 +256,13 @@
         P("tp"),
     )
     out_specs = (
-        P(("ctx", "tp"), None),
-        P("ctx", "tp"),
-        P("ctx", "tp"),
+        P(("ctx_hi", "ctx_lo", "tp"), None),
+        P(ctx, "tp"),
+        P(ctx, "tp"),
         P("tp", None),
         P("tp"),
         P("tp", None, None),
     )
     return jax.shard_map(
-        on_device, mesh=mesh, in_specs=in_specs, out_specs=out_specs, check_vma=False
-    )
+        on_device, mesh=split_mesh, in_specs=in_specs, out_specs=out_specs, check_vma=False
+    )

time: 151 us -> 187 us (1.24)
  blocking collectives: 48.5 us -> 64.7 us
  waiting for transfers between devices: 26.3 us -> 40.8 us
  local copies, waits for them, and re-layouts: 17.1 us -> 19.4 us
    all_to_all x2 -> x4, blocking collectives: 48.5 us -> 64.7 us  [the longest x2 36.6 us: ctx_exchange(): lax.all_to_all(staged, 'ctx_lo', split_axis=1, concat_axis=1, tiled=True)]
    all_to_all x1 -> x2, waiting for transfers between devices: 26.3 us -> 40.8 us  [the longest x1 26.7 us: ctx_exchange(): lax.all_to_all(staged, 'ctx_lo', split_axis=1, concat_axis=1, tiled=True)]
    all_to_all x2 -> x6, local copies, waits for them, and re-layouts: 0.65 us -> 3.18 us  [the longest x4 2.73 us: ctx_exchange(): lax.all_to_all(staged, 'ctx_lo', split_axis=1, concat_axis=1, tiled=True)]
    unnamed x17 -> x20, local copies, waits for them, and re-layouts: 9.01 us -> 9.99 us
    all_to_all x1 -> x2, starting transfers between devices: 13.7 us -> 14.5 us  [the longest x1 8.47 us: ctx_exchange(): lax.all_to_all(staged, 'ctx_lo', split_axis=1, concat_axis=1, tiled=True)]
  transfers between devices with their start and end apart: 2 -> 3, of which waited for: 1 -> 2; matrix products, arithmetic and copies ran while one was open for 11% -> 10% of each run, Pallas kernels for 0% -> 0%
where the time goes in v3:
time: 187 us; the launch traced here: 186 us
  blocking collectives  64.7 us (35%)
  waiting for transfers between devices  40.8 us (22%)
  local copies, waits for them, and re-layouts  19.4 us (10%)
  matrix products  19.1 us (10%)
  starting transfers between devices  14.5 us (8%)
  between operations  14.5 us (8%)
  other arithmetic  12.9 us (7%)
    all_to_all x2, blocking collectives, ctx_exchange(): lax.all_to_all(staged, 'ctx_lo', split_axis=1, concat_axis=1, tiled=True)  36.6 us
    all_to_all x2, blocking collectives, ctx_exchange(): lax.all_to_all(staged, 'ctx_hi', split_axis=0, concat_axis=0, tiled=True)  28.1 us
    all_to_all x1, waiting for transfers between devices, ctx_exchange(): lax.all_to_all(staged, 'ctx_lo', split_axis=1, concat_axis=1, tiled=True)  26.7 us
    all_to_all x1, waiting for transfers between devices, ctx_exchange(): lax.all_to_all(staged, 'ctx_hi', split_axis=0, concat_axis=0, tiled=True)  14.1 us
    unnamed x20, local copies, waits for them, and re-layouts  9.99 us
    all_to_all x1, starting transfers between devices, ctx_exchange(): lax.all_to_all(staged, 'ctx_lo', split_axis=1, concat_axis=1, tiled=True)  8.47 us
    all_to_all x1, starting transfers between devices, ctx_exchange(): lax.all_to_all(staged, 'ctx_hi', split_axis=0, concat_axis=0, tiled=True)  6.03 us
    reduce_sum x1, other arithmetic, blocked_backward(): carried = jnp.sum(carry_mat * ends[:, :, None, :], axis=3)  5.84 us
  transfers between devices with their start and end apart: 3, of which 2 were waited for; matrix products, arithmetic and copies ran while one was open for 10% of the time, Pallas kernels for 0%

profile of v3, /device:TPU:8, one launch (start us, length us, event | category | flops | bytes accessed | tf_op | source)
XLA Modules:
  0.0 186.1 jit_solution(8251369132313703704)
XLA Ops:
  7.2 1.1 copy.89
  8.3 0.2 copy.93
  8.5 1.1 copy.90
  9.6 0.2 copy.94
  9.8 1.1 copy.91
  11.1 1.1 copy.92
  12.4 1.1 pad_maximum_fusion
  13.5 8.5 %all-to-all-start = ((bf16[8,8,4,16,128]{4,0,3,2,1:T(8,128)(2,1)}), bf16[8,8,4,16,128]{4,0,3,2,1:T(8,128)(2,1)S(1)}, u32[]{:S(2)}, u32[]{:S(2)}) async-start(bf16[8,8,4,16,128]{4,0,3,2,1:T(8,128)(2,1)} %pad_maximum_fusion), calls=%async_computation | async-start | bytes 2097152 | tf_op jit(solution)/shard_map/all_to_all | solution.py:169
  22.0 0.8 broadcast_multiply_fusion
  23.1 0.8 dynamic_slice.15
  24.0 26.7 %all-to-all-done = bf16[8,8,4,16,128]{4,0,3,2,1:T(8,128)(2,1)S(1)} async-done(((bf16[8,8,4,16,128]{4,0,3,2,1:T(8,128)(2,1)}), bf16[8,8,4,16,128]{4,0,3,2,1:T(8,128)(2,1)S(1)}, u32[]{:S(2)}, u32[]{:S(2)}) %all-to-all-start) | async-done | bytes 1048608 | tf_op jit(solution)/shard_map/all_to_all | solution.py:169
  50.7 1.7 copy.97
  52.4 6.0 %all-to-all-start.1 = ((bf16[8,8,4,16,128]{4,1,3,2,0:T(8,128)(2,1)}), bf16[8,8,4,16,128]{4,1,3,2,0:T(8,128)(2,1)S(1)}, u32[]{:S(2)}, u32[]{:S(2)}) async-start(bf16[8,8,4,16,128]{4,1,3,2,0:T(8,128)(2,1)} %copy.97), calls=%async_computation.1 | async-start | bytes 2097152 | tf_op jit(solution)/shard_map/all_to_all | solution.py:170
  58.7 1.9 %convolution_multiply_fusion.1 = f32[16,128,128]{2,1,0:T(8,128)S(1)} fusion(f32[128,128]{1,0:T(8,128)S(1)} %fusion.48, f32[16,16]{1,0:T(8,128)S(1)} %copy.101, f32[16,16]{1,0:T(8,128)S(1)} %copy.100, f32[16,16]{1,0:T(8,128)S(1)} %copy.99), kind=kOutput, calls=%fused_computation.5 | convolution fusion | flops 50692096 | bytes 1117184 | tf_op jit(solution)/shard_map/cns,cnt->cst/dot_general | solution.py:109
  60.6 14.1 %all-to-all-done.1 = bf16[8,8,4,16,128]{4,1,3,2,0:T(8,128)(2,1)S(1)} async-done(((bf16[8,8,4,16,128]{4,1,3,2,0:T(8,128)(2,1)}), bf16[8,8,4,16,128]{4,1,3,2,0:T(8,128)(2,1)S(1)}, u32[]{:S(2)}, u32[]{:S(2)}) %all-to-all-start.1) | async-done | bytes 1048608 | tf_op jit(solution)/shard_map/all_to_all | solution.py:170
  74.7 0.3 copy.119
  75.0 0.4 slice_convert_fusion.2
  75.5 0.2 pad_slice_fusion.4
  75.7 0.2 pad_slice_fusion.5
  75.9 0.2 pad_slice_fusion.8
  76.1 0.2 pad_slice_fusion.9
  76.4 0.2 pad_slice_fusion.10
  76.6 0.2 pad_slice_fusion.11
  76.8 1.4 multiply_reduce_fusion.11
  78.2 1.0 fusion.28
  79.2 1.0 fusion.21
  80.1 5.8 %multiply_reduce_fusion.1 = (f32[16,16,64]{2,1,0:T(8,128)S(1)}, f32[16,16,64]{2,1,0:T(8,128)S(1)}) fusion(f32[16,16,64]{2,1,0:T(8,128)S(1)} %fusion.21, f32[64,64]{1,0:T(8,128)S(1)} %fusion.49, f32[16,16]{1,0:T(8,128)S(1)} %copy.102, pred[64,64]{1,0:T(8,128)(4,1)S(1)} %fusion.50, f32[16,16,64]{2,1,0:T(8,128)S(1)} %fusion.28), kind=kLoop, calls=%fused_computation.1 | loop fusion | flops 6258688 | bytes 283648 | tf_op jit(solution)/shard_map/reduce_sum | solution.py:121
  86.0 1.1 fusion.19
  87.1 1.1 fusion.24
  88.2 2.1 %fusion.3 = f32[64,16,128]{2,0,1:T(8,128)S(1)} fusion(f32[16,128,64]{1,2,0:T(8,128)S(1)} %fusion.19, f32[16,128,128]{2,1,0:T(8,128)S(1)} %convolution_multiply_fusion.1, f32[64,16,128]{2,0,1:T(8,128)S(1)} %get-tuple-element.42, f32[16]{0:T(128)S(1)} %dynamic_slice.15), kind=kOutput, calls=%fused_computation.11 | convolution fusion | flops 201719808 | bytes 2621504 | tf_op jit(solution)/shard_map/kct,cst->kcs/dot_general | solution.py:126
  90.3 2.3 %multiply_reduce_fusion.10 = (f32[16]{0:T(128)S(1)}, f32[16]{0:T(128)S(1)}, f32[16]{0:T(128)S(1)}, f32[16]{0:T(128)S(1)}, f32[16]{0:T(128)S(1)}, /*index=5*/f32[...) fusion(bf16[64,4,16,128]{3,0,2,1:T(8,128)(2,1)S(1)} %bitcast.16, ...), kind=kOutput, calls=%fused_computation.53 | convolution fusion | flops 205782896 | bytes 13108288 | tf_op jit(solution)/shard_map/kcs,cst->kct/dot_general | solution.py:118
  92.8 0.2 slice.283
  93.0 0.2 slice.285
  93.3 0.2 slice.290
  93.5 0.2 slice.292
  93.9 0.2 slice.293
  94.1 0.2 slice.295
  94.3 0.4 fusion.18
  94.7 0.4 fusion.17
  95.2 0.4 fusion.16
  95.8 25.4 %all_to_all.30 = bf16[8,8,3,16,128]{4,0,3,2,1:T(8,128)(2,1)S(1)} all-to-all(bf16[8,8,3,16,128]{4,0,3,2,1:T(8,128)(2,1)S(1)} %pad_maximum_fusion.1), channel_id=1, replica_groups=mesh['ctx_hi'=8,'ctx_lo'=8,'tp'=4] {'ctx_lo'}, dimensions={1} | all-to-all | bytes 1572864 | tf_op jit(solution)/shard_map/all_to_all | solution.py:169
  121.2 0.5 copy.106
  121.7 17.4 %all_to_all.31 = bf16[8,8,3,16,128]{4,1,3,2,0:T(8,128)(2,1)S(1)} all-to-all(bf16[8,8,3,16,128]{4,1,3,2,0:T(8,128)(2,1)S(1)} %copy.106), channel_id=1, replica_groups=mesh['ctx_hi'=8,'ctx_lo'=8,'tp'=4] {'ctx_hi'}, dimensions={0} | all-to-all | bytes 1572864 | tf_op jit(solution)/shard_map/all_to_all | solution.py:170
  139.4 3.8 %convolution_convert_fusion = bf16[128,4096]{1,0:T(8,128)(2,1)} fusion(bf16[128,1024]{0,1:T(8,128)(2,1)S(1)} %bitcast.176, bf16[4096,1024]{1,0:T(8,128)(2,1)S(1)} %bitcast.170), kind=kOutput, calls=%fused_computation.3 | convolution fusion | flops 1074266112 | bytes 9699328 | tf_op jit(solution)/shard_map/dot_general | solution.py:229
  143.5 1.1 fusion.6
  144.6 1.8 convolution_multiply_fusion
  146.4 1.9 fusion.5
  148.4 0.5 reshape.153
  148.9 11.2 %all_to_all.32 = f32[8,1,3328]{2,1,0:T(1,128)S(1)} all-to-all(f32[8,1,3328]{2,1,0:T(1,128)S(1)} %reshape.153), channel_id=1, replica_groups=mesh['ctx_hi'=8,'ctx_lo'=8,'tp'=4] {'ctx_lo'}, dimensions={0} | all-to-all | bytes 212992 | tf_op jit(solution)/shard_map/all_to_all | solution.py:169
  160.1 0.5 broadcast.69
  160.6 0.9 reduce
  161.5 0.5 reshape.154
  162.1 0.5 reshape.155
  162.6 10.7 %all_to_all.33 = f32[8,1,3328]{2,1,0:T(1,128)S(1)} all-to-all(f32[8,1,3328]{2,1,0:T(1,128)S(1)} %reshape.155), channel_id=1, replica_groups=mesh['ctx_hi'=8,'ctx_lo'=8,'tp'=4] {'ctx_hi'}, dimensions={0} | all-to-all | bytes 212992 | tf_op jit(solution)/shard_map/all_to_all | solution.py:170
  173.2 0.9 reduce.1
  174.2 0.5 reshape.156
  174.7 0.2 slice.301
  174.9 0.2 slice.300
  175.1 0.2 copy.117
  175.3 0.7 reshape.151
  175.9 0.8 copy.116
  176.7 0.8 copy.115
  177.5 0.8 copy.112
  178.4 0.8 copy.113
  (56 shorter events, 2.4 us)
Async XLA Ops:
  7.2 16.7 %copy-start = (f32[1024,3,3]{0,2,1:T(4,128)S(1)}, f32[1024,3,3]{0,2,1:T(4,128)}, u32[]{:S(2)}) copy-start(f32[1024,3,3]{0,2,1:T(4,128)} %param.14) | copy-start | bytes 110596
  13.5 37.2 %all-to-all-start = ((bf16[8,8,4,16,128]{4,0,3,2,1:T(8,128)(2,1)}), bf16[8,8,4,16,128]{4,0,3,2,1:T(8,128)(2,1)S(1)}, u32[]{:S(2)}, u32[]{:S(2)}) async-start(bf16[8,8,4,16,128]{4,0,3,2,1:T(8,128)(2,1)} %pad_maximum_fusion), calls=%async_computation | async-start | bytes 2097152 | tf_op jit(solution)/shard_map/all_to_all | solution.py:169
  52.4 22.3 %all-to-all-start.1 = ((bf16[8,8,4,16,128]{4,1,3,2,0:T(8,128)(2,1)}), bf16[8,8,4,16,128]{4,1,3,2,0:T(8,128)(2,1)S(1)}, u32[]{:S(2)}, u32[]{:S(2)}) async-start(bf16[8,8,4,16,128]{4,1,3,2,0:T(8,128)(2,1)} %copy.97), calls=%async_computation.1 | async-start | bytes 2097152 | tf_op jit(solution)/shard_map/all_to_all | solution.py:170
  58.4 120.8 %reduce-scatter.2.cloned.1.call-start = ((), (), s32[]{:S(2)}) async-start(), calls=%async_computation.7 | async-start | bytes 1310720 | tf_op jit(solution)/shard_map/reduce_scatter | solution.py:233
  94.7 44.7 %slice-start = ((s8[8388608]{0:T(1024)(128)(4,1)}), s8[4194304]{0:T(1024)(128)(4,1)S(1)}, s32[]{:S(2)}) async-start(s8[8388608]{0:T(1024)(128)(4,1)} %bitcast.169), calls=%async_computation.8 | async-start | bytes 8388608
  95.7 43.7 %slice-start.1 = ((s8[8388608]{0:T(1024)(128)(4,1)}), s8[4194304]{0:T(1024)(128)(4,1)S(1)}, s32[]{:S(2)}) async-start(s8[8388608]{0:T(1024)(128)(4,1)} %bitcast.169), calls=%async_computation.9 | async-start | bytes 8388608
Sparse Core Ops, SparseCore 0:
  143.4 15.0 reduce-scatter.1

commit v4 on v1

--- a/solution.py
+++ b/solution.py
@@ -217,10 +217,20 @@
     partial_sum = lax.dot_general(
         value_grad, w_value, (((1,), (1,)), ((), ())), preferred_element_type=jnp.float32
     )
-    narrowed = lax.optimization_barrier(partial_sum.astype(jnp.bfloat16))
-    input_grad = lax.psum_scatter(
-        narrowed.astype(jnp.float32).astype(jnp.bfloat16), "tp", scatter_dimension=0, tiled=True
-    )
+    narrowed = partial_sum.astype(jnp.bfloat16)
+    groups = lax.axis_size("tp")
+    here = lax.axis_index("tp")
+    rows_each = narrowed.shape[0] // groups
+    total = lax.dynamic_slice_in_dim(narrowed, here * rows_each, rows_each, 0).astype(jnp.float32)
+    for shift in range(1, groups):
+        outgoing = lax.dynamic_slice_in_dim(
+            narrowed, lax.rem(here + shift, groups) * rows_each, rows_each, 0
+        )
+        incoming = lax.ppermute(
+            outgoing, "tp", [(i, (i + shift) % groups) for i in range(groups)]
+        )
+        total = total + incoming.astype(jnp.float32)
+    input_grad = total.astype(jnp.bfloat16)
     return (input_grad, query_grad, key_grad, d_residues, d_skip, d_taps)
 
 

time: 151 us -> 143 us (0.947)
  blocking collectives: 48.5 us -> 0 us
  waiting for transfers between devices: 26.3 us -> 58 us
  starting transfers between devices: 13.7 us -> 28.9 us
  between operations: 14.5 us -> 1.08 us
  matrix products: 18.6 us -> 21 us
  local copies, waits for them, and re-layouts: 17.1 us -> 19.5 us
  other arithmetic: 11.9 us -> 13.9 us
    all_to_all x2 -> x0, blocking collectives: 48.5 us -> none  [the longest x1 30.1 us: on_device(): lax.all_to_all(rounded, 'ctx', split_axis=0, concat_axis=0, tiled=True)]
    all_to_all x0 -> x2, waiting for transfers between devices: none -> 31.6 us  [the longest x1 18.9 us: on_device(): lax.all_to_all(rounded, 'ctx', split_axis=0, concat_axis=0, tiled=True)]
    all_to_all x0 -> x2, starting transfers between devices: none -> 12.1 us  [the longest x1 6.26 us: on_device(): lax.all_to_all(rounded, 'ctx', split_axis=0, concat_axis=0, tiled=True)]
    ppermute x0 -> x3, starting transfers between devices: none -> 3.1 us  [on_device(): lax.ppermute(outgoing, 'tp', [(i, (i + shift) % groups) for i in range(gr...]
    dot_general x1, matrix products: 3.84 us -> 6.28 us  [on_device(): lax.dot_general(value_grad, w_value, (((1,), (1,)), ((), ())), preferred_...]
    convert_element_type x0 -> x1, other arithmetic: none -> 1.95 us  [on_device(): input_grad = total.astype(jnp.bfloat16)]
    unnamed x17 -> x13, local copies, waits for them, and re-layouts: 9.01 us -> 9.66 us
  transfers between devices with their start and end apart: 2 -> 6, of which waited for: 1 -> 3; matrix products, arithmetic and copies ran while one was open for 11% -> 12% of each run, Pallas kernels for 0% -> 0%
where the time goes in v4:
time: 143 us; the launch traced here: 142 us
  waiting for transfers between devices  58 us (41%)
  starting transfers between devices  28.9 us (20%)
  matrix products  21 us (15%)
  local copies, waits for them, and re-layouts  19.5 us (14%)
  other arithmetic  13.9 us (10%)
    all_to_all x1, waiting for transfers between devices, on_device(): lax.all_to_all(stacked_in, 'ctx', split_axis=0, concat_axis=0, tiled=True)  26.4 us
    all_to_all x1, waiting for transfers between devices, on_device(): lax.all_to_all(rounded, 'ctx', split_axis=0, concat_axis=0, tiled=True)  18.9 us
    all_to_all x1, starting transfers between devices, on_device(): lax.all_to_all(stacked_in, 'ctx', split_axis=0, concat_axis=0, tiled=True)  13.7 us
    all_to_all x1, waiting for transfers between devices, on_device(): lax.all_to_all(spread, 'ctx', split_axis=0, concat_axis=0, tiled=True)  12.7 us
    unnamed x13, local copies, waits for them, and re-layouts  9.66 us
    dot_general x1, matrix products, on_device(): lax.dot_general(value_grad, w_value, (((1,), (1,)), ((), ())), preferred_...  6.28 us
    all_to_all x1, starting transfers between devices, on_device(): lax.all_to_all(rounded, 'ctx', split_axis=0, concat_axis=0, tiled=True)  6.26 us
    all_to_all x1, starting transfers between devices, on_device(): lax.all_to_all(spread, 'ctx', split_axis=0, concat_axis=0, tiled=True)  5.85 us
  transfers between devices with their start and end apart: 6, of which 3 were waited for; matrix products, arithmetic and copies ran while one was open for 12% of the time, Pallas kernels for 0%

profile of v4, /device:TPU:8, one launch (start us, length us, event | category | flops | bytes accessed | tf_op | source)
XLA Modules:
  0.0 142.3 jit_solution(3279611953891373172)
XLA Ops:
  0.6 1.1 copy.76
  1.8 1.1 copy.77
  2.9 1.1 copy.78
  4.0 1.1 copy.79
  5.2 0.1 pad_maximum_fusion
  5.3 1.3 copy.80
  6.6 13.7 %all-to-all-start = ((bf16[64,4,16,128]{3,2,1,0:T(8,128)(2,1)}), bf16[64,4,16,128]{3,2,1,0:T(8,128)(2,1)S(1)}, u32[]{:S(2)}, u32[]{:S(2)}) async-start(bf16[64,4,16,128]{3,2,1,0:T(8,128)(2,1)} %copy.80), calls=%async_computation | async-start | bytes 2097152 | tf_op jit(solution)/shard_map/all_to_all | solution.py:179
  20.3 0.8 broadcast_multiply_fusion
  21.2 0.8 dynamic_slice.27
  22.5 1.9 %convolution_multiply_fusion.1 = f32[16,128,128]{2,1,0:T(8,128)S(1)} fusion(f32[128,128]{1,0:T(8,128)S(1)} %fusion.48, f32[16,16]{1,0:T(8,128)S(1)} %copy.84, f32[16,16]{1,0:T(8,128)S(1)} %copy.83, f32[16,16]{1,0:T(8,128)S(1)} %copy.82), kind=kOutput, calls=%fused_computation.5 | convolution fusion | flops 50692096 | bytes 1117184 | tf_op jit(solution)/shard_map/cns,cnt->cst/dot_general | solution.py:109
  24.4 26.4 %all-to-all-done = bf16[64,4,16,128]{3,2,1,0:T(8,128)(2,1)S(1)} async-done(((bf16[64,4,16,128]{3,2,1,0:T(8,128)(2,1)}), bf16[64,4,16,128]{3,2,1,0:T(8,128)(2,1)S(1)}, u32[]{:S(2)}, u32[]{:S(2)}) %all-to-all-start) | async-done | bytes 1048608 | tf_op jit(solution)/shard_map/all_to_all | solution.py:179
  50.8 0.2 fusion.51
  51.0 0.1 copy_convert_fusion.2
  51.2 0.2 pad_slice_fusion.10
  51.4 0.2 pad_slice_fusion.11
  51.6 0.3 copy_convert_fusion
  51.9 0.2 pad_slice_fusion.4
  52.1 0.2 pad_slice_fusion.5
  52.3 0.2 pad_slice_fusion.8
  52.5 0.2 pad_slice_fusion.9
  52.8 1.5 %multiply_reduce_fusion.11 = (f32[16]{0:T(128)S(1)}, f32[64,16,128]{2,0,1:T(8,128)S(1)}, f32[64,16,128]{2,0,1:T(8,128)S(1)}, f32[64,16,128]{2,0,1:T(8,128)S(1)}, f32[64,16,128]{2,0,1:T(8,128)S(1)}) fusion(f32[64,16,126]{2,0,1:T(8,128)S(1)} %bitcast.148, f32[64,16,2]{2,0,1:T(8,128)S(1)} %pad_slice_fusion.4, f32[16]{0:T(128)S(1)} %get-tuple-element.81, ...), kind=kLoop, calls=%fused_computation.54 | loop fusion | flops 3801072 | bytes 6292096 | tf_op jit(solution)/shard_map/reduce_sum | solution.py:140
  54.3 1.0 fusion.28
  55.3 1.0 fusion.21
  56.3 5.8 %multiply_reduce_fusion.1 = (f32[16,16,64]{2,1,0:T(8,128)S(1)}, f32[16,16,64]{2,1,0:T(8,128)S(1)}) fusion(f32[16,16,64]{2,1,0:T(8,128)S(1)} %fusion.21, f32[64,64]{1,0:T(8,128)S(1)} %fusion.49, f32[16,16]{1,0:T(8,128)S(1)} %copy.87, pred[64,64]{1,0:T(8,128)(4,1)S(1)} %fusion.50, f32[16,16,64]{2,1,0:T(8,128)S(1)} %fusion.28), kind=kLoop, calls=%fused_computation.1 | loop fusion | flops 6258688 | bytes 283648 | tf_op jit(solution)/shard_map/reduce_sum | solution.py:121
  62.1 1.1 fusion.19
  63.2 2.8 %multiply_reduce_fusion.7 = (f32[16]{0:T(128)S(1)}, f32[16]{0:T(128)S(1)}, f32[16]{0:T(128)S(1)}, f32[64,16,128]{2,0,1:T(8,128)S(1)}, f32[16]{0:T(128)S(1)}, /*i...) fusion(bf16[64,1,16,128]{3,2,1,0:T(8,128)(2,1)S(1)} %get-tuple-element.53, ...), kind=kOutput, calls=%fused_computation.50 | convolution fusion | flops 204341152 | bytes 6816192 | tf_op jit(solution)/shard_map/kct,cst->kcs/dot_general | solution.py:126
  66.3 1.1 fusion.24
  67.4 1.1 fusion.4
  68.7 0.2 slice.285
  68.9 0.2 slice.283
  69.1 0.2 slice.292
  69.3 0.2 slice.290
  69.5 0.2 slice.293
  69.7 0.2 slice.295
  69.9 1.1 multiply_reduce_fusion.10
  71.0 0.4 fusion.17
  71.4 0.4 fusion.16
  71.9 1.4 copy.89
  73.3 6.3 %all-to-all-start.1 = ((bf16[64,3,16,128]{3,2,1,0:T(8,128)(2,1)}), bf16[64,3,16,128]{3,2,1,0:T(8,128)(2,1)S(1)}, u32[]{:S(2)}, u32[]{:S(2)}) async-start(bf16[64,3,16,128]{3,2,1,0:T(8,128)(2,1)} %copy.89), calls=%async_computation.1 | async-start | bytes 1572864 | tf_op jit(solution)/shard_map/all_to_all | solution.py:196
  79.8 1.1 fusion.6
  80.9 1.8 %convolution_multiply_fusion = f32[16,128,128]{2,1,0:T(8,128)S(1)} fusion(f32[64,16,128]{2,0,1:T(8,128)S(1)} %get-tuple-element.43, f32[64,16,128]{2,0,1:T(8,128)S(1)} %get-tuple-element.42, f32[128,128]{1,0:T(8,128)S(1)} %fusion.48), kind=kOutput, calls=%fused_computation.4 | convolution fusion | flops 201588736 | bytes 2162688 | tf_op jit(solution)/shard_map/kcs,kct->cst/dot_general | solution.py:135
  82.7 1.9 %fusion.5 = f32[16,16]{1,0:T(8,128)S(1)} fusion(f32[16,128,128]{2,1,0:T(8,128)S(1)} %convolution_multiply_fusion, f32[16,16]{1,0:T(8,128)S(1)} %copy.84, f32[16,16]{1,0:T(8,128)S(1)} %copy.83), kind=kOutput, calls=%fused_computation.15 | convolution fusion | flops 50462464 | bytes 1051648 | tf_op jit(solution)/shard_map/cst,cnt->cns/dot_general | solution.py:136
  84.6 18.9 %all-to-all-done.1 = bf16[64,3,16,128]{3,2,1,0:T(8,128)(2,1)S(1)} async-done(((bf16[64,3,16,128]{3,2,1,0:T(8,128)(2,1)}), bf16[64,3,16,128]{3,2,1,0:T(8,128)(2,1)S(1)}, u32[]{:S(2)}, u32[]{:S(2)}) %all-to-all-start.1) | async-done | bytes 786464 | tf_op jit(solution)/shard_map/all_to_all | solution.py:196
  103.4 0.1 copy.135
  103.6 0.1 fusion.52
  103.7 6.3 %convolution_convert_fusion = bf16[128,4096]{1,0:T(8,128)(2,1)S(1)} fusion(bf16[128,1024]{0,1:T(8,128)(2,1)S(1)} %bitcast.164, bf16[4096,1024]{1,0:T(8,128)(2,1)} %param.13), kind=kOutput, calls=%fused_computation.3 | convolution fusion | flops 1074266112 | bytes 9699328 | tf_op jit(solution)/shard_map/dot_general | solution.py:217
  110.0 0.8 constant_dynamic-slice_fusion.2
  110.8 1.7 %collective-permute-start.2 = (bf16[32,4096]{1,0:T(8,128)(2,1)}, bf16[32,4096]{1,0:T(8,128)(2,1)}, u32[]{:S(2)}, u32[]{:S(2)}) collective-permute-start(bf16[32,4096]{1,0:T(8,128)(2,1)} %get-tuple-element.51), channel_id=1, source_target_pairs={{0,3},{1,0},{2,1},{3,2},{4,7},{5,4},{6,5},{7,6},{8,11},{9,8},{10,9... | collective-permute-start | bytes 786440 | tf_op jit(solution)/shard_map/ppermute | solution.py:229
  112.6 1.3 collective-permute-start.1
  114.1 1.3 reshape.126
  115.4 5.9 %all-to-all-start.2 = ((f32[64,1,416]{2,1,0:T(1,128)}), f32[64,1,416]{2,1,0:T(1,128)S(1)}, u32[]{:S(2)}, u32[]{:S(2)}) async-start(f32[64,1,416]{2,1,0:T(1,128)} %reshape.126), calls=%async_computation.2 | async-start | bytes 262144 | tf_op jit(solution)/shard_map/all_to_all | solution.py:211
  121.3 12.7 %all-to-all-done.2 = f32[64,1,416]{2,1,0:T(1,128)S(1)} async-done(((f32[64,1,416]{2,1,0:T(1,128)}), f32[64,1,416]{2,1,0:T(1,128)S(1)}, u32[]{:S(2)}, u32[]{:S(2)}) %all-to-all-start.2) | async-done | bytes 106528 | tf_op jit(solution)/shard_map/all_to_all | solution.py:211
  134.0 0.5 broadcast.71
  134.5 1.0 reduce
  135.5 0.3 reshape.127
  135.8 0.2 slice.300
  136.0 0.2 slice.301
  136.2 0.8 copy.101
  137.0 0.8 copy.102
  137.8 0.2 copy.103
  138.0 0.7 reshape.124
  138.6 0.8 copy.95
  139.5 0.8 copy.94
  140.3 2.0 %add_convert_fusion = bf16[32,4096]{1,0:T(8,128)(2,1)} fusion(bf16[32,4096]{1,0:T(8,128)(2,1)} %collective-permute-done.2, bf16[32,4096]{1,0:T(8,128)(2,1)} %collective-permute-done.1, bf16[32,4096]{1,0:T(8,128)(2,1)} %collective-permute-done, bf16[128,4096]{1,0:T(8,128)(2,1)S(1)} %convolution_convert_fusion, s32[]{:T(128)S(6)} %select_n.24), kind=kLoop, calls=%fused_computation.55 | loop fusion | flops 1048576 | bytes 1310724 | tf_op jit(solution)/shard_map/convert_element_type | solution.py:233
  (45 shorter events, 1.5 us)
Async XLA Ops:
  0.6 21.6 %copy-start = (f32[1024,3,3]{0,2,1:T(4,128)S(1)}, f32[1024,3,3]{0,2,1:T(4,128)}, u32[]{:S(2)}) copy-start(f32[1024,3,3]{0,2,1:T(4,128)} %param.14) | copy-start | bytes 110596
  6.6 44.2 %all-to-all-start = ((bf16[64,4,16,128]{3,2,1,0:T(8,128)(2,1)}), bf16[64,4,16,128]{3,2,1,0:T(8,128)(2,1)S(1)}, u32[]{:S(2)}, u32[]{:S(2)}) async-start(bf16[64,4,16,128]{3,2,1,0:T(8,128)(2,1)} %copy.80), calls=%async_computation | async-start | bytes 2097152 | tf_op jit(solution)/shard_map/all_to_all | solution.py:179
  73.3 30.2 %all-to-all-start.1 = ((bf16[64,3,16,128]{3,2,1,0:T(8,128)(2,1)}), bf16[64,3,16,128]{3,2,1,0:T(8,128)(2,1)S(1)}, u32[]{:S(2)}, u32[]{:S(2)}) async-start(bf16[64,3,16,128]{3,2,1,0:T(8,128)(2,1)} %copy.89), calls=%async_computation.1 | async-start | bytes 1572864 | tf_op jit(solution)/shard_map/all_to_all | solution.py:196
  110.8 29.5 %collective-permute-start = (bf16[32,4096]{1,0:T(8,128)(2,1)}, bf16[32,4096]{1,0:T(8,128)(2,1)}, u32[]{:S(2)}, u32[]{:S(2)}) collective-permute-start(bf16[32,4096]{1,0:T(8,128)(2,1)} %get-tuple-element.50), channel_id=1, source_target_pairs={{0,1},{1,2},{2,3},{3,0},{4,5},{5,6},{6,7},{7,4},{8,9},{9,10},{10,1... | collective-permute-start | bytes 786440 | tf_op jit(solution)/shard_map/ppermute | solution.py:229
  110.8 29.5 %collective-permute-start.2 = (bf16[32,4096]{1,0:T(8,128)(2,1)}, bf16[32,4096]{1,0:T(8,128)(2,1)}, u32[]{:S(2)}, u32[]{:S(2)}) collective-permute-start(bf16[32,4096]{1,0:T(8,128)(2,1)} %get-tuple-element.51), channel_id=1, source_target_pairs={{0,3},{1,0},{2,1},{3,2},{4,7},{5,4},{6,5},{7,6},{8,11},{9,8},{10,9... | collective-permute-start | bytes 786440 | tf_op jit(solution)/shard_map/ppermute | solution.py:229
  112.6 27.8 %collective-permute-start.1 = (bf16[32,4096]{1,0:T(8,128)(2,1)S(1)}, bf16[32,4096]{1,0:T(8,128)(2,1)}, u32[]{:S(2)}, u32[]{:S(2)}) collective-permute-start(bf16[32,4096]{1,0:T(8,128)(2,1)S(1)} %get-tuple-element.52), channel_id=1, source_target_pairs={{0,2},{1,3},{2,0},{3,1},{4,6},{5,7},{6,4},{7,5},{8,10},{9,11},{10,... | collective-permute-start | bytes 786440 | tf_op jit(solution)/shard_map/ppermute | solution.py:229
  115.4 18.6 %all-to-all-start.2 = ((f32[64,1,416]{2,1,0:T(1,128)}), f32[64,1,416]{2,1,0:T(1,128)S(1)}, u32[]{:S(2)}, u32[]{:S(2)}) async-start(f32[64,1,416]{2,1,0:T(1,128)} %reshape.126), calls=%async_computation.2 | async-start | bytes 262144 | tf_op jit(solution)/shard_map/all_to_all | solution.py:211

commit v5 on v4

--- a/solution.py
+++ b/solution.py
@@ -208,6 +208,7 @@
         axis=1,
     )
     spread = jnp.broadcast_to(packed[None], (owners,) + packed.shape)
+    query_grad, key_grad, spread = lax.optimization_barrier((query_grad, key_grad, spread))
     everyone = lax.all_to_all(spread, "ctx", split_axis=0, concat_axis=0, tiled=True)
     everyone = everyone.reshape(owners * local_rows, packed.shape[1])
     mode_count = part_residues.shape[1]

time: 143 us -> 141 us (0.986)
  waiting for transfers between devices: 58 us -> 56.3 us
    all_to_all x1, waiting for transfers between devices: 12.7 us -> 11 us  [on_device(): lax.all_to_all(spread, 'ctx', split_axis=0, concat_axis=0, tiled=True)]
where the time goes in v5:
time: 141 us; the launch traced here: 140 us
  waiting for transfers between devices  56.3 us (40%)
  starting transfers between devices  28.9 us (20%)
  matrix products  21 us (15%)
  local copies, waits for them, and re-layouts  19.4 us (14%)
  other arithmetic  13.8 us (10%)
    all_to_all x1, waiting for transfers between devices, on_device(): lax.all_to_all(stacked_in, 'ctx', split_axis=0, concat_axis=0, tiled=True)  26.4 us
    all_to_all x1, waiting for transfers between devices, on_device(): lax.all_to_all(rounded, 'ctx', split_axis=0, concat_axis=0, tiled=True)  18.9 us
    all_to_all x1, starting transfers between devices, on_device(): lax.all_to_all(stacked_in, 'ctx', split_axis=0, concat_axis=0, tiled=True)  13.7 us
    all_to_all x1, waiting for transfers between devices, on_device(): lax.all_to_all(spread, 'ctx', split_axis=0, concat_axis=0, tiled=True)  11 us
    unnamed x13, local copies, waits for them, and re-layouts  9.65 us
    dot_general x1, matrix products, on_device(): lax.dot_general(value_grad, w_value, (((1,), (1,)), ((), ())), preferred_...  6.28 us
    all_to_all x1, starting transfers between devices, on_device(): lax.all_to_all(rounded, 'ctx', split_axis=0, concat_axis=0, tiled=True)  6.26 us
    all_to_all x1, starting transfers between devices, on_device(): lax.all_to_all(spread, 'ctx', split_axis=0, concat_axis=0, tiled=True)  5.85 us
  transfers between devices with their start and end apart: 6, of which 3 were waited for; matrix products, arithmetic and copies ran while one was open for 12% of the time, Pallas kernels for 0%

profile of v5, /device:TPU:8, one launch (start us, length us, event | category | flops | bytes accessed | tf_op | source)
XLA Modules:
  0.0 140.4 jit_solution(8095527093322585465)
XLA Ops:
  0.6 1.1 copy.76
  1.8 1.1 copy.77
  2.9 1.1 copy.78
  4.0 1.1 copy.79
  5.2 0.1 pad_maximum_fusion
  5.3 1.3 copy.80
  6.6 13.7 %all-to-all-start = ((bf16[64,4,16,128]{3,2,1,0:T(8,128)(2,1)}), bf16[64,4,16,128]{3,2,1,0:T(8,128)(2,1)S(1)}, u32[]{:S(2)}, u32[]{:S(2)}) async-start(bf16[64,4,16,128]{3,2,1,0:T(8,128)(2,1)} %copy.80), calls=%async_computation | async-start | bytes 2097152 | tf_op jit(solution)/shard_map/all_to_all | solution.py:179
  20.3 0.8 broadcast_multiply_fusion
  21.2 0.8 dynamic_slice.27
  22.5 1.9 %convolution_multiply_fusion.1 = f32[16,128,128]{2,1,0:T(8,128)S(1)} fusion(f32[128,128]{1,0:T(8,128)S(1)} %fusion.48, f32[16,16]{1,0:T(8,128)S(1)} %copy.84, f32[16,16]{1,0:T(8,128)S(1)} %copy.83, f32[16,16]{1,0:T(8,128)S(1)} %copy.82), kind=kOutput, calls=%fused_computation.5 | convolution fusion | flops 50692096 | bytes 1117184 | tf_op jit(solution)/shard_map/cns,cnt->cst/dot_general | solution.py:109
  24.4 26.4 %all-to-all-done = bf16[64,4,16,128]{3,2,1,0:T(8,128)(2,1)S(1)} async-done(((bf16[64,4,16,128]{3,2,1,0:T(8,128)(2,1)}), bf16[64,4,16,128]{3,2,1,0:T(8,128)(2,1)S(1)}, u32[]{:S(2)}, u32[]{:S(2)}) %all-to-all-start) | async-done | bytes 1048608 | tf_op jit(solution)/shard_map/all_to_all | solution.py:179
  50.8 0.2 fusion.51
  51.0 0.1 copy_convert_fusion.2
  51.2 0.2 pad_slice_fusion.10
  51.4 0.2 pad_slice_fusion.11
  51.6 0.3 copy_convert_fusion
  51.9 0.2 pad_slice_fusion.4
  52.1 0.2 pad_slice_fusion.5
  52.3 0.2 pad_slice_fusion.8
  52.5 0.2 pad_slice_fusion.9
  52.8 1.5 %multiply_reduce_fusion.11 = (f32[16]{0:T(128)S(1)}, f32[64,16,128]{2,0,1:T(8,128)S(1)}, f32[64,16,128]{2,0,1:T(8,128)S(1)}, f32[64,16,128]{2,0,1:T(8,128)S(1)}, f32[64,16,128]{2,0,1:T(8,128)S(1)}) fusion(f32[64,16,126]{2,0,1:T(8,128)S(1)} %bitcast.148, f32[64,16,2]{2,0,1:T(8,128)S(1)} %pad_slice_fusion.4, f32[16]{0:T(128)S(1)} %get-tuple-element.87, ...), kind=kLoop, calls=%fused_computation.54 | loop fusion | flops 3801072 | bytes 6292096 | tf_op jit(solution)/shard_map/reduce_sum | solution.py:140
  54.3 1.0 fusion.28
  55.3 1.0 fusion.21
  56.3 5.8 %multiply_reduce_fusion.1 = (f32[16,16,64]{2,1,0:T(8,128)S(1)}, f32[16,16,64]{2,1,0:T(8,128)S(1)}) fusion(f32[16,16,64]{2,1,0:T(8,128)S(1)} %fusion.21, f32[64,64]{1,0:T(8,128)S(1)} %fusion.49, f32[16,16]{1,0:T(8,128)S(1)} %copy.87, pred[64,64]{1,0:T(8,128)(4,1)S(1)} %fusion.50, f32[16,16,64]{2,1,0:T(8,128)S(1)} %fusion.28), kind=kLoop, calls=%fused_computation.1 | loop fusion | flops 6258688 | bytes 283648 | tf_op jit(solution)/shard_map/reduce_sum | solution.py:121
  62.1 1.1 fusion.19
  63.2 2.8 %multiply_reduce_fusion.7 = (f32[16]{0:T(128)S(1)}, f32[16]{0:T(128)S(1)}, f32[16]{0:T(128)S(1)}, f32[64,16,128]{2,0,1:T(8,128)S(1)}, f32[16]{0:T(128)S(1)}, /*i...) fusion(bf16[64,1,16,128]{3,2,1,0:T(8,128)(2,1)S(1)} %get-tuple-element.59, ...), kind=kOutput, calls=%fused_computation.50 | convolution fusion | flops 204341152 | bytes 6816192 | tf_op jit(solution)/shard_map/kct,cst->kcs/dot_general | solution.py:126
  66.3 1.1 fusion.24
  67.4 1.1 fusion.4
  68.7 0.2 slice.285
  68.9 0.2 slice.283
  69.1 0.2 slice.292
  69.3 0.2 slice.290
  69.5 0.2 slice.293
  69.7 0.2 slice.295
  69.9 1.1 multiply_reduce_fusion.10
  71.0 0.4 fusion.17
  71.4 0.4 fusion.16
  71.9 1.4 copy.89
  73.3 6.3 %all-to-all-start.1 = ((bf16[64,3,16,128]{3,2,1,0:T(8,128)(2,1)}), bf16[64,3,16,128]{3,2,1,0:T(8,128)(2,1)S(1)}, u32[]{:S(2)}, u32[]{:S(2)}) async-start(bf16[64,3,16,128]{3,2,1,0:T(8,128)(2,1)} %copy.89), calls=%async_computation.1 | async-start | bytes 1572864 | tf_op jit(solution)/shard_map/all_to_all | solution.py:196
  79.8 1.1 fusion.6
  80.9 1.8 %convolution_multiply_fusion = f32[16,128,128]{2,1,0:T(8,128)S(1)} fusion(f32[64,16,128]{2,0,1:T(8,128)S(1)} %get-tuple-element.49, f32[64,16,128]{2,0,1:T(8,128)S(1)} %get-tuple-element.48, f32[128,128]{1,0:T(8,128)S(1)} %fusion.48), kind=kOutput, calls=%fused_computation.4 | convolution fusion | flops 201588736 | bytes 2162688 | tf_op jit(solution)/shard_map/kcs,kct->cst/dot_general | solution.py:135
  82.7 1.9 %fusion.5 = f32[16,16]{1,0:T(8,128)S(1)} fusion(f32[16,128,128]{2,1,0:T(8,128)S(1)} %convolution_multiply_fusion, f32[16,16]{1,0:T(8,128)S(1)} %copy.84, f32[16,16]{1,0:T(8,128)S(1)} %copy.83), kind=kOutput, calls=%fused_computation.15 | convolution fusion | flops 50462464 | bytes 1051648 | tf_op jit(solution)/shard_map/cst,cnt->cns/dot_general | solution.py:136
  84.6 18.9 %all-to-all-done.1 = bf16[64,3,16,128]{3,2,1,0:T(8,128)(2,1)S(1)} async-done(((bf16[64,3,16,128]{3,2,1,0:T(8,128)(2,1)}), bf16[64,3,16,128]{3,2,1,0:T(8,128)(2,1)S(1)}, u32[]{:S(2)}, u32[]{:S(2)}) %all-to-all-start.1) | async-done | bytes 786464 | tf_op jit(solution)/shard_map/all_to_all | solution.py:196
  103.4 0.1 copy.135
  103.6 0.1 fusion.52
  103.7 6.3 %convolution_convert_fusion = bf16[128,4096]{1,0:T(8,128)(2,1)S(1)} fusion(bf16[128,1024]{0,1:T(8,128)(2,1)S(1)} %bitcast.164, bf16[4096,1024]{1,0:T(8,128)(2,1)} %param.13), kind=kOutput, calls=%fused_computation.3 | convolution fusion | flops 1074266112 | bytes 9699328 | tf_op jit(solution)/shard_map/dot_general | solution.py:218
  110.0 0.8 constant_dynamic-slice_fusion.2
  110.8 1.7 %collective-permute-start.2 = (bf16[32,4096]{1,0:T(8,128)(2,1)S(1)}, bf16[32,4096]{1,0:T(8,128)(2,1)}, u32[]{:S(2)}, u32[]{:S(2)}) collective-permute-start(bf16[32,4096]{1,0:T(8,128)(2,1)S(1)} %get-tuple-element.57), channel_id=1, source_target_pairs={{0,3},{1,0},{2,1},{3,2},{4,7},{5,4},{6,5},{7,6},{8,11},{9,8},{10,9... | collective-permute-start | bytes 786440 | tf_op jit(solution)/shard_map/ppermute | solution.py:230
  112.5 1.3 collective-permute-start.1
  114.0 1.3 reshape.126
  115.3 5.9 %all-to-all-start.2 = ((f32[64,1,416]{2,1,0:T(1,128)}), f32[64,1,416]{2,1,0:T(1,128)S(1)}, u32[]{:S(2)}, u32[]{:S(2)}) async-start(f32[64,1,416]{2,1,0:T(1,128)} %reshape.126), calls=%async_computation.2 | async-start | bytes 262144 | tf_op jit(solution)/shard_map/all_to_all | solution.py:212
  121.2 0.9 copy.94
  122.0 0.8 copy.95
  122.9 11.0 %all-to-all-done.2 = f32[64,1,416]{2,1,0:T(1,128)S(1)} async-done(((f32[64,1,416]{2,1,0:T(1,128)}), f32[64,1,416]{2,1,0:T(1,128)S(1)}, u32[]{:S(2)}, u32[]{:S(2)}) %all-to-all-start.2) | async-done | bytes 106528 | tf_op jit(solution)/shard_map/all_to_all | solution.py:212
  133.9 0.5 broadcast.71
  134.4 1.0 reduce
  135.4 0.3 reshape.127
  135.7 0.2 slice.300
  135.9 0.2 slice.301
  136.1 0.8 copy.101
  136.9 0.8 copy.102
  137.7 0.2 copy.103
  137.9 0.7 reshape.124
  138.6 1.9 %add_convert_fusion = bf16[32,4096]{1,0:T(8,128)(2,1)} fusion(bf16[32,4096]{1,0:T(8,128)(2,1)} %collective-permute-done.2, bf16[32,4096]{1,0:T(8,128)(2,1)} %collective-permute-done.1, bf16[32,4096]{1,0:T(8,128)(2,1)S(1)} %collective-permute-done, bf16[128,4096]{1,0:T(8,128)(2,1)S(1)} %convolution_convert_fusion, s32[]{:T(128)S(6)} %select_n.24), kind=kLoop, calls=%fused_computation.55 | loop fusion | flops 1048576 | bytes 1310724 | tf_op jit(solution)/shard_map/convert_element_type | solution.py:234
  (45 shorter events, 1.5 us)
Async XLA Ops:
  0.6 21.6 %copy-start = (f32[1024,3,3]{0,2,1:T(4,128)S(1)}, f32[1024,3,3]{0,2,1:T(4,128)}, u32[]{:S(2)}) copy-start(f32[1024,3,3]{0,2,1:T(4,128)} %param.14) | copy-start | bytes 110596
  6.6 44.2 %all-to-all-start = ((bf16[64,4,16,128]{3,2,1,0:T(8,128)(2,1)}), bf16[64,4,16,128]{3,2,1,0:T(8,128)(2,1)S(1)}, u32[]{:S(2)}, u32[]{:S(2)}) async-start(bf16[64,4,16,128]{3,2,1,0:T(8,128)(2,1)} %copy.80), calls=%async_computation | async-start | bytes 2097152 | tf_op jit(solution)/shard_map/all_to_all | solution.py:179
  73.3 30.2 %all-to-all-start.1 = ((bf16[64,3,16,128]{3,2,1,0:T(8,128)(2,1)}), bf16[64,3,16,128]{3,2,1,0:T(8,128)(2,1)S(1)}, u32[]{:S(2)}, u32[]{:S(2)}) async-start(bf16[64,3,16,128]{3,2,1,0:T(8,128)(2,1)} %copy.89), calls=%async_computation.1 | async-start | bytes 1572864 | tf_op jit(solution)/shard_map/all_to_all | solution.py:196
  110.8 27.8 %collective-permute-start = (bf16[32,4096]{1,0:T(8,128)(2,1)}, bf16[32,4096]{1,0:T(8,128)(2,1)S(1)}, u32[]{:S(2)}, u32[]{:S(2)}) collective-permute-start(bf16[32,4096]{1,0:T(8,128)(2,1)} %get-tuple-element.56), channel_id=1, source_target_pairs={{0,1},{1,2},{2,3},{3,0},{4,5},{5,6},{6,7},{7,4},{8,9},{9,10},{10,1... | collective-permute-start | bytes 786440 | tf_op jit(solution)/shard_map/ppermute | solution.py:230
  110.8 27.8 %collective-permute-start.2 = (bf16[32,4096]{1,0:T(8,128)(2,1)S(1)}, bf16[32,4096]{1,0:T(8,128)(2,1)}, u32[]{:S(2)}, u32[]{:S(2)}) collective-permute-start(bf16[32,4096]{1,0:T(8,128)(2,1)S(1)} %get-tuple-element.57), channel_id=1, source_target_pairs={{0,3},{1,0},{2,1},{3,2},{4,7},{5,4},{6,5},{7,6},{8,11},{9,8},{10,9... | collective-permute-start | bytes 786440 | tf_op jit(solution)/shard_map/ppermute | solution.py:230
  112.5 26.0 %collective-permute-start.1 = (bf16[32,4096]{1,0:T(8,128)(2,1)S(1)}, bf16[32,4096]{1,0:T(8,128)(2,1)}, u32[]{:S(2)}, u32[]{:S(2)}) collective-permute-start(bf16[32,4096]{1,0:T(8,128)(2,1)S(1)} %get-tuple-element.58), channel_id=1, source_target_pairs={{0,2},{1,3},{2,0},{3,1},{4,6},{5,7},{6,4},{7,5},{8,10},{9,11},{10,... | collective-permute-start | bytes 786440 | tf_op jit(solution)/shard_map/ppermute | solution.py:230
  115.3 18.6 %all-to-all-start.2 = ((f32[64,1,416]{2,1,0:T(1,128)}), f32[64,1,416]{2,1,0:T(1,128)S(1)}, u32[]{:S(2)}, u32[]{:S(2)}) async-start(f32[64,1,416]{2,1,0:T(1,128)} %reshape.126), calls=%async_computation.2 | async-start | bytes 262144 | tf_op jit(solution)/shard_map/all_to_all | solution.py:212

commit v6 on v5

--- a/solution.py
+++ b/solution.py
@@ -215,20 +215,19 @@
     d_residues = everyone[:, :mode_count]
     d_skip = everyone[:, mode_count]
     d_taps = everyone[:, mode_count + 1 :].reshape(-1, part_taps.shape[0], tap_count)
-    partial_sum = lax.dot_general(
-        value_grad, w_value, (((1,), (1,)), ((), ())), preferred_element_type=jnp.float32
-    )
-    narrowed = partial_sum.astype(jnp.bfloat16)
     groups = lax.axis_size("tp")
     here = lax.axis_index("tp")
-    rows_each = narrowed.shape[0] // groups
-    total = lax.dynamic_slice_in_dim(narrowed, here * rows_each, rows_each, 0).astype(jnp.float32)
+    rows_each = value_grad.shape[0] // groups
+    rolled = jnp.roll(value_grad.reshape(groups, rows_each, -1), -here, axis=0)
+    partial_sum = lax.dot_general(
+        rolled.reshape(value_grad.shape), w_value, (((1,), (1,)), ((), ())),
+        preferred_element_type=jnp.float32,
+    )
+    narrowed = partial_sum.astype(jnp.bfloat16).reshape(groups, rows_each, -1)
+    total = narrowed[0].astype(jnp.float32)
     for shift in range(1, groups):
-        outgoing = lax.dynamic_slice_in_dim(
-            narrowed, lax.rem(here + shift, groups) * rows_each, rows_each, 0
-        )
         incoming = lax.ppermute(
-            outgoing, "tp", [(i, (i + shift) % groups) for i in range(groups)]
+            narrowed[shift], "tp", [(i, (i + shift) % groups) for i in range(groups)]
         )
         total = total + incoming.astype(jnp.float32)
     input_grad = total.astype(jnp.bfloat16)

time: 141 us -> 141 us (level)
  no operation moved by 1% of the time
where the time goes in v6:
time: 141 us
  waiting for transfers between devices  56.3 us (40%)
  starting transfers between devices  28.9 us (20%)
  matrix products  21 us (15%)
  local copies, waits for them, and re-layouts  20.5 us (15%)
  other arithmetic  12.9 us (9%)
    all_to_all x1, waiting for transfers between devices, on_device(): lax.all_to_all(stacked_in, 'ctx', split_axis=0, concat_axis=0, tiled=True)  26.4 us
    all_to_all x1, waiting for transfers between devices, on_device(): lax.all_to_all(rounded, 'ctx', split_axis=0, concat_axis=0, tiled=True)  18.9 us
    all_to_all x1, starting transfers between devices, on_device(): lax.all_to_all(stacked_in, 'ctx', split_axis=0, concat_axis=0, tiled=True)  13.7 us
    all_to_all x1, waiting for transfers between devices, on_device(): lax.all_to_all(spread, 'ctx', split_axis=0, concat_axis=0, tiled=True)  11 us
    unnamed x13, local copies, waits for them, and re-layouts  9.65 us
    all_to_all x1, starting transfers between devices, on_device(): lax.all_to_all(rounded, 'ctx', split_axis=0, concat_axis=0, tiled=True)  6.26 us
    dot_general x1, matrix products, on_device(): lax.dot_general(rolled.reshape(value_grad.shape), w_value, (((1,), (1,)),...  6.23 us
    all_to_all x1, starting transfers between devices, on_device(): lax.all_to_all(spread, 'ctx', split_axis=0, concat_axis=0, tiled=True)  5.86 us
  transfers between devices with their start and end apart: 6, of which 3 were waited for; matrix products, arithmetic and copies ran while one was open for 12% of the time, Pallas kernels for 0%

profile of v6, /device:TPU:8, one launch (start us, length us, event | category | flops | bytes accessed | tf_op | source)
XLA Modules:
  0.0 140.6 jit_solution(8238013474092127534)
XLA Ops:
  0.6 1.1 copy.98
  1.8 1.1 copy.99
  2.9 1.1 copy.100
  4.0 1.1 copy.101
  5.3 1.3 copy.102
  6.6 13.7 %all-to-all-start = ((bf16[64,4,16,128]{3,2,1,0:T(8,128)(2,1)}), bf16[64,4,16,128]{3,2,1,0:T(8,128)(2,1)S(1)}, u32[]{:S(2)}, u32[]{:S(2)}) async-start(bf16[64,4,16,128]{3,2,1,0:T(8,128)(2,1)} %copy.102), calls=%async_computation | async-start | bytes 2097152 | tf_op jit(solution)/shard_map/all_to_all | solution.py:179
  20.3 0.8 broadcast_multiply_fusion
  21.2 0.8 dynamic_slice.19
  22.5 1.9 %convolution_multiply_fusion.1 = f32[16,128,128]{2,1,0:T(8,128)S(1)} fusion(f32[128,128]{1,0:T(8,128)S(1)} %fusion.49, f32[16,16]{1,0:T(8,128)S(1)} %copy.106, f32[16,16]{1,0:T(8,128)S(1)} %copy.105, f32[16,16]{1,0:T(8,128)S(1)} %copy.104), kind=kOutput, calls=%fused_computation.5 | convolution fusion | flops 50692096 | bytes 1117184 | tf_op jit(solution)/shard_map/cns,cnt->cst/dot_general | solution.py:109
  24.4 26.4 %all-to-all-done = bf16[64,4,16,128]{3,2,1,0:T(8,128)(2,1)S(1)} async-done(((bf16[64,4,16,128]{3,2,1,0:T(8,128)(2,1)}), bf16[64,4,16,128]{3,2,1,0:T(8,128)(2,1)S(1)}, u32[]{:S(2)}, u32[]{:S(2)}) %all-to-all-start) | async-done | bytes 1048608 | tf_op jit(solution)/shard_map/all_to_all | solution.py:179
  50.8 0.2 fusion.53
  51.2 0.2 pad_slice_fusion.10
  51.4 0.2 pad_slice_fusion.11
  51.6 0.3 copy_convert_fusion
  51.9 0.2 pad_slice_fusion.4
  52.1 0.2 pad_slice_fusion.5
  52.3 0.2 pad_slice_fusion.8
  52.5 0.2 pad_slice_fusion.9
  52.8 1.5 %multiply_reduce_fusion.11 = (f32[16]{0:T(128)S(1)}, f32[64,16,128]{2,0,1:T(8,128)S(1)}, f32[64,16,128]{2,0,1:T(8,128)S(1)}, f32[64,16,128]{2,0,1:T(8,128)S(1)}, f32[64,16,128]{2,0,1:T(8,128)S(1)}) fusion(f32[64,16,126]{2,0,1:T(8,128)S(1)} %bitcast.152, f32[64,16,2]{2,0,1:T(8,128)S(1)} %pad_slice_fusion.4, f32[16]{0:T(128)S(1)} %get-tuple-element.93, ...), kind=kLoop, calls=%fused_computation.56 | loop fusion | flops 3801072 | bytes 6292096 | tf_op jit(solution)/shard_map/reduce_sum | solution.py:140
  54.3 1.0 fusion.29
  55.3 1.0 fusion.22
  56.3 5.8 %multiply_reduce_fusion.1 = (f32[16,16,64]{2,1,0:T(8,128)S(1)}, f32[16,16,64]{2,1,0:T(8,128)S(1)}) fusion(f32[16,16,64]{2,1,0:T(8,128)S(1)} %fusion.22, f32[64,64]{1,0:T(8,128)S(1)} %fusion.50, f32[16,16]{1,0:T(8,128)S(1)} %copy.109, pred[64,64]{1,0:T(8,128)(4,1)S(1)} %fusion.51, f32[16,16,64]{2,1,0:T(8,128)S(1)} %fusion.29), kind=kLoop, calls=%fused_computation.1 | loop fusion | flops 6258688 | bytes 283648 | tf_op jit(solution)/shard_map/reduce_sum | solution.py:121
  62.1 1.1 fusion.20
  63.2 2.8 %multiply_reduce_fusion.7 = (f32[16]{0:T(128)S(1)}, f32[16]{0:T(128)S(1)}, f32[16]{0:T(128)S(1)}, f32[64,16,128]{2,0,1:T(8,128)S(1)}, f32[16]{0:T(128)S(1)}, /*i...) fusion(bf16[64,1,16,128]{3,2,1,0:T(8,128)(2,1)S(1)} %get-tuple-element.65, ...), kind=kOutput, calls=%fused_computation.52 | convolution fusion | flops 204341152 | bytes 6816192 | tf_op jit(solution)/shard_map/kct,cst->kcs/dot_general | solution.py:126
  66.3 1.1 fusion.25
  67.4 1.1 fusion.4
  68.7 0.2 slice.305
  68.9 0.2 slice.303
  69.1 0.2 slice.312
  69.3 0.2 slice.310
  69.5 0.2 slice.313
  69.7 0.2 slice.315
  69.9 1.1 multiply_reduce_fusion.10
  71.0 0.4 fusion.18
  71.4 0.4 fusion.17
  71.9 1.4 copy.111
  73.3 6.3 %all-to-all-start.1 = ((bf16[64,3,16,128]{3,2,1,0:T(8,128)(2,1)}), bf16[64,3,16,128]{3,2,1,0:T(8,128)(2,1)S(1)}, u32[]{:S(2)}, u32[]{:S(2)}) async-start(bf16[64,3,16,128]{3,2,1,0:T(8,128)(2,1)} %copy.111), calls=%async_computation.1 | async-start | bytes 1572864 | tf_op jit(solution)/shard_map/all_to_all | solution.py:196
  79.8 1.1 fusion.6
  80.9 1.8 %convolution_multiply_fusion = f32[16,128,128]{2,1,0:T(8,128)S(1)} fusion(f32[64,16,128]{2,0,1:T(8,128)S(1)} %get-tuple-element.55, f32[64,16,128]{2,0,1:T(8,128)S(1)} %get-tuple-element.54, f32[128,128]{1,0:T(8,128)S(1)} %fusion.49), kind=kOutput, calls=%fused_computation.4 | convolution fusion | flops 201588736 | bytes 2162688 | tf_op jit(solution)/shard_map/kcs,kct->cst/dot_general | solution.py:135
  82.7 1.9 %fusion.5 = f32[16,16]{1,0:T(8,128)S(1)} fusion(f32[16,128,128]{2,1,0:T(8,128)S(1)} %convolution_multiply_fusion, f32[16,16]{1,0:T(8,128)S(1)} %copy.106, f32[16,16]{1,0:T(8,128)S(1)} %copy.105), kind=kOutput, calls=%fused_computation.15 | convolution fusion | flops 50462464 | bytes 1051648 | tf_op jit(solution)/shard_map/cst,cnt->cns/dot_general | solution.py:136
  84.6 18.9 %all-to-all-done.1 = bf16[64,3,16,128]{3,2,1,0:T(8,128)(2,1)S(1)} async-done(((bf16[64,3,16,128]{3,2,1,0:T(8,128)(2,1)}), bf16[64,3,16,128]{3,2,1,0:T(8,128)(2,1)S(1)}, u32[]{:S(2)}, u32[]{:S(2)}) %all-to-all-start.1) | async-done | bytes 786464 | tf_op jit(solution)/shard_map/all_to_all | solution.py:196
  103.4 0.1 copy.159
  103.6 0.1 fusion.54
  103.7 0.4 reshape_squeeze.3
  104.1 0.6 copy.113
  104.8 6.2 %convolution_convert_fusion = bf16[128,4096]{1,0:T(8,128)(2,1)S(1)} fusion(bf16[128,1024]{1,0:T(8,128)(2,1)S(1)} %bitcast.168, bf16[4096,1024]{1,0:T(8,128)(2,1)} %param.13), kind=kOutput, calls=%fused_computation.3 | convolution fusion | flops 1074266112 | bytes 9699328 | tf_op jit(solution)/shard_map/dot_general | solution.py:222
  111.1 0.9 fusion.52
  112.0 1.7 %collective-permute-start.2 = (bf16[32,4096]{1,0:T(8,128)(2,1)}, bf16[32,4096]{1,0:T(8,128)(2,1)S(1)}, u32[]{:S(2)}, u32[]{:S(2)}) collective-permute-start(bf16[32,4096]{1,0:T(8,128)(2,1)} %get-tuple-element.63), channel_id=1, source_target_pairs={{0,3},{1,0},{2,1},{3,2},{4,7},{5,4},{6,5},{7,6},{8,11},{9,8},{10,9... | collective-permute-start | bytes 786440 | tf_op jit(solution)/shard_map/ppermute | solution.py:229
  113.7 1.3 collective-permute-start.1
  115.2 1.3 reshape.139
  116.5 5.9 %all-to-all-start.2 = ((f32[64,1,416]{2,1,0:T(1,128)}), f32[64,1,416]{2,1,0:T(1,128)S(1)}, u32[]{:S(2)}, u32[]{:S(2)}) async-start(f32[64,1,416]{2,1,0:T(1,128)} %reshape.139), calls=%async_computation.2 | async-start | bytes 262144 | tf_op jit(solution)/shard_map/all_to_all | solution.py:212
  122.4 0.9 copy.118
  123.3 0.8 copy.119
  124.1 11.0 %all-to-all-done.2 = f32[64,1,416]{2,1,0:T(1,128)S(1)} async-done(((f32[64,1,416]{2,1,0:T(1,128)}), f32[64,1,416]{2,1,0:T(1,128)S(1)}, u32[]{:S(2)}, u32[]{:S(2)}) %all-to-all-start.2) | async-done | bytes 106528 | tf_op jit(solution)/shard_map/all_to_all | solution.py:212
  135.1 0.5 broadcast.69
  135.6 1.0 reduce
  136.6 0.3 reshape.140
  136.9 0.2 slice.324
  137.1 0.2 slice.325
  137.3 0.8 copy.125
  138.1 0.8 copy.126
  138.9 0.2 copy.127
  139.1 0.7 reshape.137
  139.8 0.8 add_convert_fusion
  (48 shorter events, 1.9 us)
Async XLA Ops:
  0.6 21.6 %copy-start = (f32[1024,3,3]{0,2,1:T(4,128)S(1)}, f32[1024,3,3]{0,2,1:T(4,128)}, u32[]{:S(2)}) copy-start(f32[1024,3,3]{0,2,1:T(4,128)} %param.14) | copy-start | bytes 110596
  6.6 44.2 %all-to-all-start = ((bf16[64,4,16,128]{3,2,1,0:T(8,128)(2,1)}), bf16[64,4,16,128]{3,2,1,0:T(8,128)(2,1)S(1)}, u32[]{:S(2)}, u32[]{:S(2)}) async-start(bf16[64,4,16,128]{3,2,1,0:T(8,128)(2,1)} %copy.102), calls=%async_computation | async-start | bytes 2097152 | tf_op jit(solution)/shard_map/all_to_all | solution.py:179
  73.3 30.2 %all-to-all-start.1 = ((bf16[64,3,16,128]{3,2,1,0:T(8,128)(2,1)}), bf16[64,3,16,128]{3,2,1,0:T(8,128)(2,1)S(1)}, u32[]{:S(2)}, u32[]{:S(2)}) async-start(bf16[64,3,16,128]{3,2,1,0:T(8,128)(2,1)} %copy.111), calls=%async_computation.1 | async-start | bytes 1572864 | tf_op jit(solution)/shard_map/all_to_all | solution.py:196
  112.0 27.8 %collective-permute-start = (bf16[32,4096]{1,0:T(8,128)(2,1)}, bf16[32,4096]{1,0:T(8,128)(2,1)S(1)}, u32[]{:S(2)}, u32[]{:S(2)}) collective-permute-start(bf16[32,4096]{1,0:T(8,128)(2,1)} %get-tuple-element.62), channel_id=1, source_target_pairs={{0,1},{1,2},{2,3},{3,0},{4,5},{5,6},{6,7},{7,4},{8,9},{9,10},{10,1... | collective-permute-start | bytes 786440 | tf_op jit(solution)/shard_map/ppermute | solution.py:229
  112.0 27.8 %collective-permute-start.2 = (bf16[32,4096]{1,0:T(8,128)(2,1)}, bf16[32,4096]{1,0:T(8,128)(2,1)S(1)}, u32[]{:S(2)}, u32[]{:S(2)}) collective-permute-start(bf16[32,4096]{1,0:T(8,128)(2,1)} %get-tuple-element.63), channel_id=1, source_target_pairs={{0,3},{1,0},{2,1},{3,2},{4,7},{5,4},{6,5},{7,6},{8,11},{9,8},{10,9... | collective-permute-start | bytes 786440 | tf_op jit(solution)/shard_map/ppermute | solution.py:229
  113.7 26.1 %collective-permute-start.1 = (bf16[32,4096]{1,0:T(8,128)(2,1)}, bf16[32,4096]{1,0:T(8,128)(2,1)S(1)}, u32[]{:S(2)}, u32[]{:S(2)}) collective-permute-start(bf16[32,4096]{1,0:T(8,128)(2,1)} %get-tuple-element.64), channel_id=1, source_target_pairs={{0,2},{1,3},{2,0},{3,1},{4,6},{5,7},{6,4},{7,5},{8,10},{9,11},{10,... | collective-permute-start | bytes 786440 | tf_op jit(solution)/shard_map/ppermute | solution.py:229
  116.5 18.6 %all-to-all-start.2 = ((f32[64,1,416]{2,1,0:T(1,128)}), f32[64,1,416]{2,1,0:T(1,128)S(1)}, u32[]{:S(2)}, u32[]{:S(2)}) async-start(f32[64,1,416]{2,1,0:T(1,128)} %reshape.139), calls=%async_computation.2 | async-start | bytes 262144 | tf_op jit(solution)/shard_map/all_to_all | solution.py:212

commit v7 on v6

--- a/solution.py
+++ b/solution.py
@@ -111,32 +111,36 @@
 
     idx = jnp.arange(blocks, dtype=jnp.float32)
     gap = idx[:, None] - 1.0 - idx[None, :]
+    rate_flat = rate_table.reshape(-1)
+    modes = rate_table.shape[1]
     carry_mat = jnp.where(
-        gap >= 0, jnp.exp(-rate[..., None] * block_len * jnp.maximum(gap, 0.0)), 0.0
+        gap[..., None] >= 0,
+        jnp.exp(-rate_flat * block_len * jnp.maximum(gap, 0.0)[..., None]),
+        0.0,
     )
 
     conv_intra = jnp.einsum("kcs,cst->kct", xb, toeplitz, precision=highest)
     tail_w = jnp.exp(-rate * (block_len - 1 - offs))
-    ends = jnp.einsum("kcs,cns->cnk", xb, tail_w, precision=highest)
-    carried = jnp.sum(carry_mat * ends[:, :, None, :], axis=3)
+    ends = jnp.einsum("kcs,cns->kcn", xb, tail_w, precision=highest).reshape(blocks, -1)
+    carried = jnp.sum(carry_mat * ends[None, :, :], axis=1).reshape(blocks, chans, modes)
     lead_w = residue_table[:, :, None] * jnp.exp(-rate * (offs + 1.0))
-    conv_carry = jnp.einsum("cnk,cnt->kct", carried, lead_w, precision=highest)
+    conv_carry = jnp.einsum("kcn,cnt->kct", carried, lead_w, precision=highest)
     conv_out = conv_intra + conv_carry
 
     back_intra = jnp.einsum("kct,cst->kcs", gb, toeplitz, precision=highest)
-    starts = jnp.einsum("kct,cnt->cnk", gb, up, precision=highest)
-    later = jnp.sum(carry_mat * starts[:, :, :, None], axis=2)
+    starts = jnp.einsum("kct,cnt->kcn", gb, up, precision=highest).reshape(blocks, -1)
+    later = jnp.sum(carry_mat * starts[:, None, :], axis=0).reshape(blocks, chans, modes)
     back_w = jnp.exp(-rate * (block_len - offs))
     back_carry = jnp.einsum(
-        "cnk,cns->kcs", later, residue_table[:, :, None] * back_w, precision=highest
+        "kcn,cns->kcs", later, residue_table[:, :, None] * back_w, precision=highest
     )
     grad_mixed = back_intra + back_carry + skip_b * gb
 
     pairs = jnp.einsum("kcs,kct->cst", xb, gb, precision=highest) * tri
     paired = jnp.einsum("cst,cnt->cns", pairs, up, precision=highest)
     res_intra = jnp.sum(paired * down, axis=2)
-    lead_sums = jnp.einsum("kcs,cns->cnk", xb, back_w, precision=highest)
-    grad_residues = res_intra + jnp.sum(later * lead_sums, axis=2)
+    lead_sums = jnp.einsum("kcs,cns->kcn", xb, back_w, precision=highest)
+    grad_residues = res_intra + jnp.sum(later * lead_sums, axis=0)
     grad_skip = jnp.sum(gb * xb, axis=(0, 2))
 
     grad_query = cotangent * (conv_out + skip_b * xb)

time: 141 us -> 149 us (1.057)
  local copies, waits for them, and re-layouts: 20.5 us -> 26.6 us
  matrix products: 21 us -> 26.8 us
  waiting for transfers between devices: 56.3 us -> 50.7 us
    all_to_all x1, waiting for transfers between devices: 26.4 us -> 20.9 us  [on_device(): lax.all_to_all(stacked_in, 'ctx', split_axis=0, concat_axis=0, tiled=True)]
    slice x6, local copies, waits for them, and re-layouts: 0.24 us -> 3.39 us  [advance(): nxt[:, :, :amount]]
    dot_general x1, matrix products: 2.78 us -> 5.82 us  [blocked_backward(): back_intra = jnp.einsum('kct,cst->kcs', gb, toeplitz, precision=highest)]
    reduce_sum x1, other arithmetic: 5.84 us -> 3.46 us  [blocked_backward(): jnp.sum(carry_mat * ends[None, :, :], axis=1).reshape(blocks, chans, modes)]
    unnamed x13 -> x111, local copies, waits for them, and re-layouts: 9.65 us -> 9.87 us
  transfers between devices with their start and end apart: 6 -> 6, of which waited for: 3 -> 3; matrix products, arithmetic and copies ran while one was open for 12% -> 15% of each run, Pallas kernels for 0% -> 0%
where the time goes in v7:
time: 149 us
  waiting for transfers between devices  50.7 us (34%)
  starting transfers between devices  28.9 us (19%)
  matrix products  26.8 us (18%)
  local copies, waits for them, and re-layouts  26.6 us (18%)
  other arithmetic  13.9 us (9%)
  between operations  1.72 us (1%)
    all_to_all x1, waiting for transfers between devices, on_device(): lax.all_to_all(stacked_in, 'ctx', split_axis=0, concat_axis=0, tiled=True)  20.9 us
    all_to_all x1, waiting for transfers between devices, on_device(): lax.all_to_all(rounded, 'ctx', split_axis=0, concat_axis=0, tiled=True)  18.8 us
    all_to_all x1, starting transfers between devices, on_device(): lax.all_to_all(stacked_in, 'ctx', split_axis=0, concat_axis=0, tiled=True)  13.7 us
    all_to_all x1, waiting for transfers between devices, on_device(): lax.all_to_all(spread, 'ctx', split_axis=0, concat_axis=0, tiled=True)  11 us
    unnamed x111, local copies, waits for them, and re-layouts  9.87 us
    all_to_all x1, starting transfers between devices, on_device(): lax.all_to_all(rounded, 'ctx', split_axis=0, concat_axis=0, tiled=True)  6.26 us
    dot_general x1, matrix products, on_device(): lax.dot_general(rolled.reshape(value_grad.shape), w_value, (((1,), (1,)),...  6.24 us
    all_to_all x1, starting transfers between devices, on_device(): lax.all_to_all(spread, 'ctx', split_axis=0, concat_axis=0, tiled=True)  5.86 us
  transfers between devices with their start and end apart: 6, of which 3 were waited for; matrix products, arithmetic and copies ran while one was open for 15% of the time, Pallas kernels for 0%

profile of v7, /device:TPU:8, one launch (start us, length us, event | category | flops | bytes accessed | tf_op | source)
XLA Modules:
  0.0 148.7 jit_solution(9359144564929263344)
XLA Ops:
  0.6 1.1 copy.133
  1.8 1.1 copy.134
  2.9 1.1 copy.135
  4.0 1.1 copy.136
  5.3 1.3 copy.137
  6.6 13.7 %all-to-all-start = ((bf16[64,4,16,128]{3,2,1,0:T(8,128)(2,1)}), bf16[64,4,16,128]{3,2,1,0:T(8,128)(2,1)S(1)}, u32[]{:S(2)}, u32[]{:S(2)}) async-start(bf16[64,4,16,128]{3,2,1,0:T(8,128)(2,1)} %copy.137), calls=%async_computation | async-start | bytes 2097152 | tf_op jit(solution)/shard_map/all_to_all | solution.py:183
  20.3 0.8 broadcast_multiply_fusion
  21.1 1.4 dynamic_slice.19
  22.6 0.6 mul.390
  23.3 0.5 iota_subtract_fusion.1
  23.9 0.5 iota_add_fusion.1
  24.4 0.5 iota_subtract_fusion.2
  25.0 0.6 slice_bitcast_fusion.14
  25.6 0.6 slice_bitcast_fusion.10
  26.3 0.7 fusion.51
  27.0 2.9 %convolution_multiply_fusion.1 = f32[16,128,128]{2,1,0:T(8,128)} fusion(f32[128,128]{1,0:T(8,128)S(1)} %fusion.50, f32[16,16]{1,0:T(8,128)S(1)} %copy.141, f32[16,16]{1,0:T(8,128)S(1)} %copy.140, f32[16,16]{1,0:T(8,128)S(1)} %copy.139), kind=kOutput, calls=%fused_computation.5 | convolution fusion | flops 50692096 | bytes 1117184 | tf_op jit(solution)/shard_map/cns,cnt->cst/dot_general | solution.py:109
  29.9 20.9 %all-to-all-done = bf16[64,4,16,128]{3,2,1,0:T(8,128)(2,1)S(1)} async-done(((bf16[64,4,16,128]{3,2,1,0:T(8,128)(2,1)}), bf16[64,4,16,128]{3,2,1,0:T(8,128)(2,1)S(1)}, u32[]{:S(2)}, u32[]{:S(2)}) %all-to-all-start) | async-done | bytes 1048608 | tf_op jit(solution)/shard_map/all_to_all | solution.py:183
  51.2 0.2 pad_slice_fusion.10
  51.7 0.2 copy_convert_fusion
  53.0 2.9 %multiply_reduce_fusion.11 = (f32[16]{0:T(128)}, f32[64,16,128]{2,0,1:T(8,128)S(1)}, f32[64,16,128]{2,0,1:T(8,128)S(1)}, f32[64,16,128]{2,0,1:T(8,128)}, f32[64,16,128]{2,0,1:T(8,128)}) fusion(f32[64,16,126]{2,0,1:T(8,128)S(1)} %bitcast.166, f32[64,16,2]{2,0,1:T(8,128)S(1)} %pad_slice_fusion.4, f32[16]{0:T(128)S(1)} %copy-done.37, ...), kind=kLoop, calls=%fused_computation.57 | loop fusion | flops 3801072 | bytes 6292096 | tf_op jit(solution)/shard_map/reduce_sum | solution.py:144
  55.9 1.0 fusion.23
  57.0 1.0 fusion.30
  58.1 3.5 %multiply_reduce_fusion.1 = (f32[64,256]{1,0:T(8,128)}, f32[64,256]{1,0:T(8,128)S(1)}) fusion(f32[64,256]{1,0:T(8,128)S(1)} %copy.145, f32[64,64]{1,0:T(8,128)} %fusion.51, f32[256]{0:T(256)} %mul.390, pred[64,64]{1,0:T(8,128)(4,1)S(1)} %fusion.52, f32[64,256]{1,0:T(8,128)S(1)} %copy.148), kind=kLoop, calls=%fused_computation.2 | loop fusion | flops 6258688 | bytes 283648 | tf_op jit(solution)/shard_map/reduce_sum | solution.py:125
  61.7 1.7 %fusion.21 = f32[16,128,64]{1,2,0:T(8,128)S(1)} fusion(f32[64,16,16]{0,2,1:T(8,128)S(1)} %bitcast.182, f32[128]{0:T(128)} %iota_subtract_fusion.1, f32[16,16]{1,0:T(8,128)S(1)} %copy.141, f32[16,16]{1,0:T(8,128)S(1)} %copy.139), kind=kOutput, calls=%fused_computation.81 | convolution fusion | flops 25231360 | bytes 592384 | tf_op jit(solution)/shard_map/kcn,cns->kcs/dot_general | solution.py:134
  63.4 5.8 %multiply_reduce_fusion.7 = (f32[16]{0:T(128)}, f32[16]{0:T(128)}, f32[16]{0:T(128)}, f32[64,16,128]{2,0,1:T(8,128)S(1)}, f32[16]{0:T(128)S(1)}, /*index=5*/f32[...) fusion(bf16[64,1,16,128]{3,2,1,0:T(8,128)(2,1)S(1)} %get-tuple-element.71, f32[64,16,126]{2,0,1:T(8,128)S(1)} %bitcast.172, ...), kind=kOutput, calls=%fused_computation.53 | convolution fusion | flops 204341152 | bytes 6816192 | tf_op jit(solution)/shard_map/kct,cst->kcs/dot_general | solution.py:130
  69.3 0.8 pad_slice_fusion
  70.1 0.8 pad_slice_fusion.1
  71.0 0.8 pad_slice_fusion.2
  71.8 0.8 pad_slice_fusion.3
  72.7 1.1 fusion.26
  73.9 2.3 %fusion.4 = f32[64,16,128]{2,0,1:T(8,128)S(1)} fusion(f32[16,128,64]{1,2,0:T(8,128)S(1)} %fusion.26, f32[16,128,128]{2,1,0:T(8,128)} %convolution_multiply_fusion.1, f32[64,16,128]{2,0,1:T(8,128)S(1)} %get-tuple-element.61, f32[16]{0:T(128)S(1)} %copy-done.42, bf16[64,1,16,128]{3,2,1,0:T(8,128)(2,1)S(1)} %copy-done.15), kind=kOutput, calls=%fused_computation.12 | convolution fusion | flops 201981952 | bytes 2883648 | tf_op jit(solution)/shard_map/kcs,cst->kct/dot_general | solution.py:122
  76.6 0.2 slice.303
  76.8 0.2 slice.312
  77.2 0.2 slice.313
  77.4 0.2 slice.315
  77.7 1.0 multiply_reduce_fusion.10
  78.8 0.4 fusion.19
  79.4 0.4 fusion.18
  79.9 1.4 copy.150
  81.3 6.3 %all-to-all-start.1 = ((bf16[64,3,16,128]{3,2,1,0:T(8,128)(2,1)}), bf16[64,3,16,128]{3,2,1,0:T(8,128)(2,1)S(1)}, u32[]{:S(2)}, u32[]{:S(2)}) async-start(bf16[64,3,16,128]{3,2,1,0:T(8,128)(2,1)} %copy.150), calls=%async_computation.1 | async-start | bytes 1572864 | tf_op jit(solution)/shard_map/all_to_all | solution.py:200
  87.9 1.1 fusion.7
  89.0 1.8 %convolution_multiply_fusion = f32[16,128,128]{2,1,0:T(8,128)S(1)} fusion(f32[64,16,128]{2,0,1:T(8,128)S(1)} %get-tuple-element.61, f32[64,16,128]{2,0,1:T(8,128)S(1)} %copy-done.2, f32[128,128]{1,0:T(8,128)S(1)} %fusion.50), kind=kOutput, calls=%fused_computation.4 | convolution fusion | flops 201588736 | bytes 2162688 | tf_op jit(solution)/shard_map/kcs,kct->cst/dot_general | solution.py:139
  90.8 1.9 %fusion.6 = f32[16,16]{1,0:T(8,128)S(1)} fusion(f32[16,128,128]{2,1,0:T(8,128)S(1)} %convolution_multiply_fusion, f32[16,16]{1,0:T(8,128)S(1)} %copy.141, f32[16,16]{1,0:T(8,128)S(1)} %copy.140), kind=kOutput, calls=%fused_computation.16 | convolution fusion | flops 50462464 | bytes 1051648 | tf_op jit(solution)/shard_map/cst,cnt->cns/dot_general | solution.py:140
  92.7 18.8 %all-to-all-done.1 = bf16[64,3,16,128]{3,2,1,0:T(8,128)(2,1)S(1)} async-done(((bf16[64,3,16,128]{3,2,1,0:T(8,128)(2,1)}), bf16[64,3,16,128]{3,2,1,0:T(8,128)(2,1)S(1)}, u32[]{:S(2)}, u32[]{:S(2)}) %all-to-all-start.1) | async-done | bytes 786464 | tf_op jit(solution)/shard_map/all_to_all | solution.py:200
  111.8 0.4 reshape_squeeze.3
  112.2 0.6 copy.152
  112.9 6.2 %convolution_convert_fusion = bf16[128,4096]{1,0:T(8,128)(2,1)S(1)} fusion(bf16[128,1024]{1,0:T(8,128)(2,1)S(1)} %bitcast.184, bf16[4096,1024]{1,0:T(8,128)(2,1)} %param.13), kind=kOutput, calls=%fused_computation | convolution fusion | flops 1074266112 | bytes 9699328 | tf_op jit(solution)/shard_map/dot_general | solution.py:226
  119.2 0.9 fusion.53
  120.0 1.7 %collective-permute-start.2 = (bf16[32,4096]{1,0:T(8,128)(2,1)}, bf16[32,4096]{1,0:T(8,128)(2,1)S(1)}, u32[]{:S(2)}, u32[]{:S(2)}) collective-permute-start(bf16[32,4096]{1,0:T(8,128)(2,1)} %get-tuple-element.69), channel_id=1, source_target_pairs={{0,3},{1,0},{2,1},{3,2},{4,7},{5,4},{6,5},{7,6},{8,11},{9,8},{10,9... | collective-permute-start | bytes 786440 | tf_op jit(solution)/shard_map/ppermute | solution.py:233
  121.8 1.3 collective-permute-start.1
  123.3 1.3 reshape.175
  124.6 5.9 %all-to-all-start.2 = ((f32[64,1,416]{2,1,0:T(1,128)}), f32[64,1,416]{2,1,0:T(1,128)S(1)}, u32[]{:S(2)}, u32[]{:S(2)}) async-start(f32[64,1,416]{2,1,0:T(1,128)} %reshape.175), calls=%async_computation.2 | async-start | bytes 262144 | tf_op jit(solution)/shard_map/all_to_all | solution.py:216
  130.5 0.9 copy.157
  131.3 0.8 copy.158
  132.2 11.0 %all-to-all-done.2 = f32[64,1,416]{2,1,0:T(1,128)S(1)} async-done(((f32[64,1,416]{2,1,0:T(1,128)}), f32[64,1,416]{2,1,0:T(1,128)S(1)}, u32[]{:S(2)}, u32[]{:S(2)}) %all-to-all-start.2) | async-done | bytes 106528 | tf_op jit(solution)/shard_map/all_to_all | solution.py:216
  143.2 0.5 broadcast.85
  143.7 1.0 reduce
  144.7 0.3 reshape.176
  145.0 0.2 slice.324
  145.2 0.2 slice.325
  145.4 0.8 copy.164
  146.2 0.8 copy.165
  147.2 0.7 reshape.173
  147.8 0.8 add_convert_fusion
  (151 shorter events, 4.2 us)
Async XLA Ops:
  0.6 24.3 %copy-start = (f32[1024,3,3]{0,2,1:T(4,128)S(1)}, f32[1024,3,3]{0,2,1:T(4,128)}, u32[]{:S(2)}) copy-start(f32[1024,3,3]{0,2,1:T(4,128)} %param.14) | copy-start | bytes 110596
  6.6 44.2 %all-to-all-start = ((bf16[64,4,16,128]{3,2,1,0:T(8,128)(2,1)}), bf16[64,4,16,128]{3,2,1,0:T(8,128)(2,1)S(1)}, u32[]{:S(2)}, u32[]{:S(2)}) async-start(bf16[64,4,16,128]{3,2,1,0:T(8,128)(2,1)} %copy.137), calls=%async_computation | async-start | bytes 2097152 | tf_op jit(solution)/shard_map/all_to_all | solution.py:183
  51.0 1.9 %copy-start.11 = (bf16[64,1,16,128]{3,2,1,0:T(8,128)(2,1)}, bf16[64,1,16,128]{3,2,1,0:T(8,128)(2,1)S(1)}, u32[]{:S(2)}) copy-start(bf16[64,1,16,128]{3,2,1,0:T(8,128)(2,1)S(1)} %get-tuple-element.72) | copy-start | bytes 786436
  51.0 1.9 %copy-start.12 = (bf16[64,1,16,128]{3,2,1,0:T(8,128)(2,1)}, bf16[64,1,16,128]{3,2,1,0:T(8,128)(2,1)S(1)}, u32[]{:S(2)}) copy-start(bf16[64,1,16,128]{3,2,1,0:T(8,128)(2,1)S(1)} %get-tuple-element.74) | copy-start | bytes 786436
  51.0 1.9 %copy-start.14 = (bf16[64,1,16,128]{3,2,1,0:T(8,128)(2,1)}, bf16[64,1,16,128]{3,2,1,0:T(8,128)(2,1)S(1)}, u32[]{:S(2)}) copy-start(bf16[64,1,16,128]{3,2,1,0:T(8,128)(2,1)S(1)} %get-tuple-element.73) | copy-start | bytes 786436
  51.4 1.5 %copy-start.7 = (f32[64,16,2]{2,0,1:T(8,128)}, f32[64,16,2]{2,0,1:T(8,128)S(1)}, u32[]{:S(2)}) copy-start(f32[64,16,2]{2,0,1:T(8,128)S(1)} %pad_slice_fusion.10) | copy-start | bytes 24580
  51.6 1.3 copy-start.8
  51.6 1.3 copy-start.23
  51.6 1.3 copy-start.25
  51.6 1.3 copy-start.27
  51.6 1.3 copy-start.29
  51.6 1.3 copy-start.31
  51.6 1.3 copy-start.33
  51.7 1.3 copy-start.35
  51.7 1.3 copy-start.37
  51.7 1.3 copy-start.39
  52.2 3.7 %copy-start.3 = (f32[64,16,2]{2,0,1:T(8,128)}, f32[64,16,2]{2,0,1:T(8,128)S(1)}, u32[]{:S(2)}) copy-start(f32[64,16,2]{2,0,1:T(8,128)S(1)} %pad_slice_fusion.4) | copy-start | bytes 24580
  52.4 3.5 %copy-start.5 = (f32[64,16,1]{2,0,1:T(8,128)}, f32[64,16,1]{2,0,1:T(8,128)S(1)}, u32[]{:S(2)}) copy-start(f32[64,16,1]{2,0,1:T(8,128)S(1)} %pad_slice_fusion.5) | copy-start | bytes 12292
  52.6 3.3 %copy-start.9 = (f32[64,16,2]{2,0,1:T(8,128)}, f32[64,16,2]{2,0,1:T(8,128)S(1)}, u32[]{:S(2)}) copy-start(f32[64,16,2]{2,0,1:T(8,128)S(1)} %pad_slice_fusion.8) | copy-start | bytes 24580
  52.9 3.1 %copy-start.10 = (f32[64,16,1]{2,0,1:T(8,128)}, f32[64,16,1]{2,0,1:T(8,128)S(1)}, u32[]{:S(2)}) copy-start(f32[64,16,1]{2,0,1:T(8,128)S(1)} %pad_slice_fusion.9) | copy-start | bytes 12292
  53.0 2.9 %copy-start.49 = (f32[128]{0:T(128)S(1)}, f32[128]{0:T(128)}, u32[]{:S(2)}) copy-start(f32[128]{0:T(128)} %iota_subtract_fusion.2) | copy-start | bytes 1540
  55.9 7.5 %copy-start.1 = (f32[64,16,128]{2,0,1:T(8,128)}, f32[64,16,128]{2,0,1:T(8,128)S(1)}, u32[]{:S(2)}) copy-start(f32[64,16,128]{2,0,1:T(8,128)S(1)} %get-tuple-element.60) | copy-start | bytes 1572868
  61.7 1.7 %copy-start.20 = (f32[64,256]{0,1:T(8,128)}, f32[64,256]{0,1:T(8,128)S(1)}, u32[]{:S(2)}) copy-start(f32[64,256]{0,1:T(8,128)S(1)} %copy.149) | copy-start | bytes 196612
  69.2 3.4 %copy-start.22 = (f32[64,256]{1,0:T(8,128)S(1)}, f32[64,256]{1,0:T(8,128)}, u32[]{:S(2)}) copy-start(f32[64,256]{1,0:T(8,128)} %get-tuple-element.57) | copy-start | bytes 196612
  69.2 3.5 %copy-start.48 = (f32[128]{0:T(128)S(1)}, f32[128]{0:T(128)}, u32[]{:S(2)}) copy-start(f32[128]{0:T(128)} %iota_add_fusion.1) | copy-start | bytes 1540
  69.2 4.7 %copy-start.15 = (bf16[64,1,16,128]{3,2,1,0:T(8,128)(2,1)S(1)}, bf16[64,1,16,128]{3,2,1,0:T(8,128)(2,1)}, u32[]{:S(2)}) copy-start(bf16[64,1,16,128]{3,2,1,0:T(8,128)(2,1)} %copy-done.14) | copy-start | bytes 786436
  69.2 4.7 %copy-start.42 = (f32[16]{0:T(128)S(1)}, f32[16]{0:T(128)}, u32[]{:S(2)}) copy-start(f32[16]{0:T(128)} %dynamic_slice.19) | copy-start | bytes 196
  76.2 1.4 copy-start.4
  76.2 1.4 copy-start.6
  76.2 1.4 copy-start.13
  76.3 1.4 copy-start.36
  76.3 1.4 copy-start.38
  76.3 1.4 copy-start.40
  77.0 1.8 %copy-start.18 = (f32[64,16,2]{2,0,1:T(8,128)S(1)}, f32[64,16,2]{2,0,1:T(8,128)}, u32[]{:S(2)}) copy-start(f32[64,16,2]{2,0,1:T(8,128)} %pad_slice_fusion.2) | copy-start | bytes 24580
  77.0 1.8 %copy-start.19 = (f32[64,16,1]{2,0,1:T(8,128)S(1)}, f32[64,16,1]{2,0,1:T(8,128)}, u32[]{:S(2)}) copy-start(f32[64,16,1]{2,0,1:T(8,128)} %pad_slice_fusion.3) | copy-start | bytes 12292
  77.0 1.8 %copy-start.30 = (f32[16]{0:T(128)S(1)}, f32[16]{0:T(128)}, u32[]{:S(2)}) copy-start(f32[16]{0:T(128)} %get-tuple-element.104) | copy-start | bytes 196
  77.0 1.8 %copy-start.32 = (f32[16]{0:T(128)S(1)}, f32[16]{0:T(128)}, u32[]{:S(2)}) copy-start(f32[16]{0:T(128)} %get-tuple-element.105) | copy-start | bytes 196
  77.0 1.8 %copy-start.34 = (f32[16]{0:T(128)S(1)}, f32[16]{0:T(128)}, u32[]{:S(2)}) copy-start(f32[16]{0:T(128)} %get-tuple-element.106) | copy-start | bytes 196
  77.7 1.6 %copy-start.16 = (f32[64,16,2]{2,0,1:T(8,128)S(1)}, f32[64,16,2]{2,0,1:T(8,128)}, u32[]{:S(2)}) copy-start(f32[64,16,2]{2,0,1:T(8,128)} %pad_slice_fusion) | copy-start | bytes 24580
  77.7 1.6 %copy-start.17 = (f32[64,16,1]{2,0,1:T(8,128)S(1)}, f32[64,16,1]{2,0,1:T(8,128)}, u32[]{:S(2)}) copy-start(f32[64,16,1]{2,0,1:T(8,128)} %pad_slice_fusion.1) | copy-start | bytes 12292
  77.7 1.6 %copy-start.24 = (f32[16]{0:T(128)S(1)}, f32[16]{0:T(128)}, u32[]{:S(2)}) copy-start(f32[16]{0:T(128)} %get-tuple-element.95) | copy-start | bytes 196
  77.7 1.6 %copy-start.26 = (f32[16]{0:T(128)S(1)}, f32[16]{0:T(128)}, u32[]{:S(2)}) copy-start(f32[16]{0:T(128)} %get-tuple-element.96) | copy-start | bytes 196
  77.7 1.6 %copy-start.28 = (f32[16]{0:T(128)S(1)}, f32[16]{0:T(128)}, u32[]{:S(2)}) copy-start(f32[16]{0:T(128)} %get-tuple-element.97) | copy-start | bytes 196
  79.3 8.3 %copy-start.43 = (f32[16]{0:T(128)S(1)}, f32[16]{0:T(128)}, u32[]{:S(2)}) copy-start(f32[16]{0:T(128)} %get-tuple-element.59) | copy-start | bytes 196
  79.3 8.4 %copy-start.45 = (f32[16]{0:T(128)S(1)}, f32[16]{0:T(128)}, u32[]{:S(2)}) copy-start(f32[16]{0:T(128)} %get-tuple-element.51) | copy-start | bytes 196
  79.3 8.4 %copy-start.46 = (f32[16]{0:T(128)S(1)}, f32[16]{0:T(128)}, u32[]{:S(2)}) copy-start(f32[16]{0:T(128)} %get-tuple-element.52) | copy-start | bytes 196
  79.4 8.4 %copy-start.47 = (f32[16]{0:T(128)S(1)}, f32[16]{0:T(128)}, u32[]{:S(2)}) copy-start(f32[16]{0:T(128)} %get-tuple-element.53) | copy-start | bytes 196
  79.4 8.4 %copy-start.44 = (f32[16]{0:T(128)S(1)}, f32[16]{0:T(128)}, u32[]{:S(2)}) copy-start(f32[16]{0:T(128)} %get-tuple-element.81) | copy-start | bytes 196
  79.4 8.5 %copy-start.21 = (f32[64,256]{0,1:T(8,128)S(1)}, f32[64,256]{0,1:T(8,128)}, u32[]{:S(2)}) copy-start(f32[64,256]{0,1:T(8,128)} %copy-done.20) | copy-start | bytes 196612
  79.4 8.5 %copy-start.41 = (f32[128]{0:T(128)S(1)}, f32[128]{0:T(128)}, u32[]{:S(2)}) copy-start(f32[128]{0:T(128)} %iota_subtract_fusion.1) | copy-start | bytes 1540
  79.4 9.6 %copy-start.2 = (f32[64,16,128]{2,0,1:T(8,128)S(1)}, f32[64,16,128]{2,0,1:T(8,128)}, u32[]{:S(2)}) copy-start(f32[64,16,128]{2,0,1:T(8,128)} %copy-done.1) | copy-start | bytes 1572868
  81.3 30.2 %all-to-all-start.1 = ((bf16[64,3,16,128]{3,2,1,0:T(8,128)(2,1)}), bf16[64,3,16,128]{3,2,1,0:T(8,128)(2,1)S(1)}, u32[]{:S(2)}, u32[]{:S(2)}) async-start(bf16[64,3,16,128]{3,2,1,0:T(8,128)(2,1)} %copy.150), calls=%async_computation.1 | async-start | bytes 1572864 | tf_op jit(solution)/shard_map/all_to_all | solution.py:200
  120.0 27.8 %collective-permute-start = (bf16[32,4096]{1,0:T(8,128)(2,1)}, bf16[32,4096]{1,0:T(8,128)(2,1)S(1)}, u32[]{:S(2)}, u32[]{:S(2)}) collective-permute-start(bf16[32,4096]{1,0:T(8,128)(2,1)} %get-tuple-element.68), channel_id=1, source_target_pairs={{0,1},{1,2},{2,3},{3,0},{4,5},{5,6},{6,7},{7,4},{8,9},{9,10},{10,1... | collective-permute-start | bytes 786440 | tf_op jit(solution)/shard_map/ppermute | solution.py:233
  120.0 27.8 %collective-permute-start.2 = (bf16[32,4096]{1,0:T(8,128)(2,1)}, bf16[32,4096]{1,0:T(8,128)(2,1)S(1)}, u32[]{:S(2)}, u32[]{:S(2)}) collective-permute-start(bf16[32,4096]{1,0:T(8,128)(2,1)} %get-tuple-element.69), channel_id=1, source_target_pairs={{0,3},{1,0},{2,1},{3,2},{4,7},{5,4},{6,5},{7,6},{8,11},{9,8},{10,9... | collective-permute-start | bytes 786440 | tf_op jit(solution)/shard_map/ppermute | solution.py:233
  121.8 26.1 %collective-permute-start.1 = (bf16[32,4096]{1,0:T(8,128)(2,1)}, bf16[32,4096]{1,0:T(8,128)(2,1)S(1)}, u32[]{:S(2)}, u32[]{:S(2)}) collective-permute-start(bf16[32,4096]{1,0:T(8,128)(2,1)} %get-tuple-element.70), channel_id=1, source_target_pairs={{0,2},{1,3},{2,0},{3,1},{4,6},{5,7},{6,4},{7,5},{8,10},{9,11},{10,... | collective-permute-start | bytes 786440 | tf_op jit(solution)/shard_map/ppermute | solution.py:233
  124.6 18.6 %all-to-all-start.2 = ((f32[64,1,416]{2,1,0:T(1,128)}), f32[64,1,416]{2,1,0:T(1,128)S(1)}, u32[]{:S(2)}, u32[]{:S(2)}) async-start(f32[64,1,416]{2,1,0:T(1,128)} %reshape.175), calls=%async_computation.2 | async-start | bytes 262144 | tf_op jit(solution)/shard_map/all_to_all | solution.py:216

commit v8 on v6

--- a/solution.py
+++ b/solution.py
@@ -207,10 +207,13 @@
         ],
         axis=1,
     )
-    spread = jnp.broadcast_to(packed[None], (owners,) + packed.shape)
+    packed_len = packed.shape[0] * packed.shape[1]
+    lane_rows = -(-packed_len // 128)
+    tiled_pack = jnp.pad(packed.reshape(-1), (0, lane_rows * 128 - packed_len)).reshape(lane_rows, 128)
+    spread = jnp.broadcast_to(tiled_pack[None], (owners, lane_rows, 128))
     query_grad, key_grad, spread = lax.optimization_barrier((query_grad, key_grad, spread))
     everyone = lax.all_to_all(spread, "ctx", split_axis=0, concat_axis=0, tiled=True)
-    everyone = everyone.reshape(owners * local_rows, packed.shape[1])
+    everyone = everyone.reshape(owners, -1)[:, :packed_len].reshape(owners * local_rows, packed.shape[1])
     mode_count = part_residues.shape[1]
     d_residues = everyone[:, :mode_count]
     d_skip = everyone[:, mode_count]

time: 141 us -> 135 us (0.957)
  waiting for transfers between devices: 56.3 us -> 51.5 us
    all_to_all x1, waiting for transfers between devices: 11 us -> 0.01 us  [on_device(): lax.all_to_all(spread, 'ctx', split_axis=0, concat_axis=0, tiled=True)]
    ppermute x3, waiting for transfers between devices: 0.01 us -> 6.47 us  [on_device(): lax.ppermute(narrowed[shift], 'tp', [(i, (i + shift) % groups) for i in r...]
    unnamed x13 -> x10, local copies, waits for them, and re-layouts: 9.65 us -> 7.02 us
  transfers between devices with their start and end apart: 6 -> 6, of which waited for: 3 -> 4; matrix products, arithmetic and copies ran while one was open for 12% -> 17% of each run, Pallas kernels for 0% -> 0%
where the time goes in v8:
time: 135 us; the launch traced here: 134 us
  waiting for transfers between devices  51.5 us (38%)
  starting transfers between devices  29 us (21%)
  matrix products  21 us (16%)
  local copies, waits for them, and re-layouts  19.4 us (14%)
  other arithmetic  11.9 us (9%)
    all_to_all x1, waiting for transfers between devices, on_device(): lax.all_to_all(stacked_in, 'ctx', split_axis=0, concat_axis=0, tiled=True)  26.4 us
    all_to_all x1, waiting for transfers between devices, on_device(): lax.all_to_all(rounded, 'ctx', split_axis=0, concat_axis=0, tiled=True)  18.7 us
    all_to_all x1, starting transfers between devices, on_device(): lax.all_to_all(stacked_in, 'ctx', split_axis=0, concat_axis=0, tiled=True)  13.7 us
    unnamed x10, local copies, waits for them, and re-layouts  7.02 us
    ppermute x3, waiting for transfers between devices, on_device(): lax.ppermute(narrowed[shift], 'tp', [(i, (i + shift) % groups) for i in r...  6.47 us
    all_to_all x1, starting transfers between devices, on_device(): lax.all_to_all(rounded, 'ctx', split_axis=0, concat_axis=0, tiled=True)  6.26 us
    dot_general x1, matrix products, on_device(): lax.dot_general(rolled.reshape(value_grad.shape), w_value, (((1,), (1,)),...  6.23 us
    all_to_all x1, starting transfers between devices, on_device(): lax.all_to_all(spread, 'ctx', split_axis=0, concat_axis=0, tiled=True)  5.93 us
  transfers between devices with their start and end apart: 6, of which 4 were waited for; matrix products, arithmetic and copies ran while one was open for 17% of the time, Pallas kernels for 0%

profile of v8, /device:TPU:8, one launch (start us, length us, event | category | flops | bytes accessed | tf_op | source)
XLA Modules:
  0.0 133.8 jit_solution(16937361804735943778)
XLA Ops:
  0.6 1.1 copy.87
  1.8 1.1 copy.88
  2.9 1.1 copy.89
  4.0 1.1 copy.90
  5.2 0.1 pad_maximum_fusion
  5.3 1.3 copy.91
  6.6 13.7 %all-to-all-start = ((bf16[64,4,16,128]{3,2,1,0:T(8,128)(2,1)}), bf16[64,4,16,128]{3,2,1,0:T(8,128)(2,1)S(1)}, u32[]{:S(2)}, u32[]{:S(2)}) async-start(bf16[64,4,16,128]{3,2,1,0:T(8,128)(2,1)} %copy.91), calls=%async_computation | async-start | bytes 2097152 | tf_op jit(solution)/shard_map/all_to_all | solution.py:179
  20.3 0.8 broadcast_multiply_fusion
  21.2 0.8 dynamic_slice.19
  22.5 1.9 %convolution_multiply_fusion.1 = f32[16,128,128]{2,1,0:T(8,128)S(1)} fusion(f32[128,128]{1,0:T(8,128)S(1)} %fusion.49, f32[16,16]{1,0:T(8,128)S(1)} %copy.95, f32[16,16]{1,0:T(8,128)S(1)} %copy.94, f32[16,16]{1,0:T(8,128)S(1)} %copy.93), kind=kOutput, calls=%fused_computation.5 | convolution fusion | flops 50692096 | bytes 1117184 | tf_op jit(solution)/shard_map/cns,cnt->cst/dot_general | solution.py:109
  24.4 26.4 %all-to-all-done = bf16[64,4,16,128]{3,2,1,0:T(8,128)(2,1)S(1)} async-done(((bf16[64,4,16,128]{3,2,1,0:T(8,128)(2,1)}), bf16[64,4,16,128]{3,2,1,0:T(8,128)(2,1)S(1)}, u32[]{:S(2)}, u32[]{:S(2)}) %all-to-all-start) | async-done | bytes 1048608 | tf_op jit(solution)/shard_map/all_to_all | solution.py:179
  50.8 0.2 fusion.53
  51.0 0.1 copy_convert_fusion.2
  51.2 0.2 pad_slice_fusion.10
  51.4 0.2 pad_slice_fusion.11
  51.6 0.3 copy_convert_fusion
  51.9 0.2 pad_slice_fusion.4
  52.1 0.2 pad_slice_fusion.5
  52.3 0.2 pad_slice_fusion.8
  52.5 0.2 pad_slice_fusion.9
  52.8 1.5 %multiply_reduce_fusion.11 = (f32[16]{0:T(128)S(1)}, f32[64,16,128]{2,0,1:T(8,128)S(1)}, f32[64,16,128]{2,0,1:T(8,128)S(1)}, f32[64,16,128]{2,0,1:T(8,128)S(1)}, f32[64,16,128]{2,0,1:T(8,128)S(1)}) fusion(f32[64,16,126]{2,0,1:T(8,128)S(1)} %bitcast.157, f32[64,16,2]{2,0,1:T(8,128)S(1)} %pad_slice_fusion.4, f32[16]{0:T(128)S(1)} %get-tuple-element.87, ...), kind=kLoop, calls=%fused_computation.57 | loop fusion | flops 3801072 | bytes 6292096 | tf_op jit(solution)/shard_map/reduce_sum | solution.py:140
  54.3 1.0 fusion.29
  55.3 1.0 fusion.22
  56.3 5.8 %multiply_reduce_fusion.1 = (f32[16,16,64]{2,1,0:T(8,128)S(1)}, f32[16,16,64]{2,1,0:T(8,128)S(1)}) fusion(f32[16,16,64]{2,1,0:T(8,128)S(1)} %fusion.22, f32[64,64]{1,0:T(8,128)S(1)} %fusion.50, f32[16,16]{1,0:T(8,128)S(1)} %copy.98, pred[64,64]{1,0:T(8,128)(4,1)S(1)} %fusion.51, f32[16,16,64]{2,1,0:T(8,128)S(1)} %fusion.29), kind=kLoop, calls=%fused_computation.1 | loop fusion | flops 6258688 | bytes 283648 | tf_op jit(solution)/shard_map/reduce_sum | solution.py:121
  62.1 1.1 fusion.20
  63.2 2.8 %multiply_reduce_fusion.7 = (f32[16]{0:T(128)S(1)}, f32[16]{0:T(128)S(1)}, f32[16]{0:T(128)S(1)}, f32[64,16,128]{2,0,1:T(8,128)S(1)}, f32[16]{0:T(128)S(1)}, /*i...) fusion(bf16[64,1,16,128]{3,2,1,0:T(8,128)(2,1)S(1)} %get-tuple-element.59, ...), kind=kOutput, calls=%fused_computation.53 | convolution fusion | flops 204341152 | bytes 6816192 | tf_op jit(solution)/shard_map/kct,cst->kcs/dot_general | solution.py:126
  66.3 1.1 fusion.25
  67.4 1.1 fusion.4
  68.7 0.2 slice.309
  68.9 0.2 slice.307
  69.1 0.2 slice.316
  69.3 0.2 slice.314
  69.5 0.2 slice.317
  69.7 0.2 slice.319
  69.9 1.1 multiply_reduce_fusion.10
  71.0 0.4 fusion.18
  71.4 0.4 fusion.17
  71.9 1.4 %copy.100 = bf16[64,3,16,128]{3,2,1,0:T(8,128)(2,1)} copy(bf16[64,3,16,128]{3,0,2,1:T(8,128)(2,1)S(1)} %pad_maximum_fusion.1) | data formatting | bytes 1572864 | tf_op jit(solution)/shard_map/stack | solution.py:161
  73.3 6.3 %all-to-all-start.1 = ((bf16[64,3,16,128]{3,2,1,0:T(8,128)(2,1)}), bf16[64,3,16,128]{3,2,1,0:T(8,128)(2,1)S(1)}, u32[]{:S(2)}, u32[]{:S(2)}) async-start(bf16[64,3,16,128]{3,2,1,0:T(8,128)(2,1)} %copy.100), calls=%async_computation.1 | async-start | bytes 1572864 | tf_op jit(solution)/shard_map/all_to_all | solution.py:196
  79.8 1.1 fusion.6
  80.9 1.8 %convolution_multiply_fusion = f32[16,128,128]{2,1,0:T(8,128)S(1)} fusion(f32[64,16,128]{2,0,1:T(8,128)S(1)} %get-tuple-element.49, f32[64,16,128]{2,0,1:T(8,128)S(1)} %get-tuple-element.48, f32[128,128]{1,0:T(8,128)S(1)} %fusion.49), kind=kOutput, calls=%fused_computation.4 | convolution fusion | flops 201588736 | bytes 2162688 | tf_op jit(solution)/shard_map/kcs,kct->cst/dot_general | solution.py:135
  82.7 1.9 %fusion.5 = f32[16,16]{1,0:T(8,128)S(1)} fusion(f32[16,128,128]{2,1,0:T(8,128)S(1)} %convolution_multiply_fusion, f32[16,16]{1,0:T(8,128)S(1)} %copy.95, f32[16,16]{1,0:T(8,128)S(1)} %copy.94), kind=kOutput, calls=%fused_computation.15 | convolution fusion | flops 50462464 | bytes 1051648 | tf_op jit(solution)/shard_map/cst,cnt->cns/dot_general | solution.py:136
  84.7 18.7 %all-to-all-done.1 = bf16[64,3,16,128]{3,2,1,0:T(8,128)(2,1)S(1)} async-done(((bf16[64,3,16,128]{3,2,1,0:T(8,128)(2,1)}), bf16[64,3,16,128]{3,2,1,0:T(8,128)(2,1)S(1)}, u32[]{:S(2)}, u32[]{:S(2)}) %all-to-all-start.1) | async-done | bytes 786464 | tf_op jit(solution)/shard_map/all_to_all | solution.py:196
  103.4 0.1 copy.147
  103.6 0.1 fusion.54
  103.7 0.7 broadcast_in_dim.18
  104.4 5.9 %all-to-all-start.2 = ((f32[64,4,128]{2,1,0:T(4,128)}), f32[64,4,128]{2,1,0:T(4,128)S(1)}, u32[]{:S(2)}, u32[]{:S(2)}) async-start(f32[64,4,128]{2,1,0:T(4,128)} %broadcast_in_dim.18), calls=%async_computation.2 | async-start | bytes 262144 | tf_op jit(solution)/shard_map/all_to_all | solution.py:215
  110.3 0.4 reshape_squeeze.3
  110.7 0.6 copy.102
  111.5 6.2 %convolution_convert_fusion = bf16[128,4096]{1,0:T(8,128)(2,1)S(1)} fusion(bf16[128,1024]{1,0:T(8,128)(2,1)S(1)} %bitcast.171, bf16[4096,1024]{1,0:T(8,128)(2,1)} %param.13), kind=kOutput, calls=%fused_computation.3 | convolution fusion | flops 1074266112 | bytes 9699328 | tf_op jit(solution)/shard_map/dot_general | solution.py:225
  117.7 0.8 fusion.52
  118.5 1.7 %collective-permute-start.2 = (bf16[32,4096]{1,0:T(8,128)(2,1)}, bf16[32,4096]{1,0:T(8,128)(2,1)S(1)}, u32[]{:S(2)}, u32[]{:S(2)}) collective-permute-start(bf16[32,4096]{1,0:T(8,128)(2,1)} %get-tuple-element.57), channel_id=1, source_target_pairs={{0,3},{1,0},{2,1},{3,2},{4,7},{5,4},{6,5},{7,6},{8,11},{9,8},{10,9... | collective-permute-start | bytes 786440 | tf_op jit(solution)/shard_map/ppermute | solution.py:232
  120.3 1.3 %collective-permute-start.1 = (bf16[32,4096]{1,0:T(8,128)(2,1)S(1)}, bf16[32,4096]{1,0:T(8,128)(2,1)S(1)}, u32[]{:S(2)}, u32[]{:S(2)}) collective-permute-start(bf16[32,4096]{1,0:T(8,128)(2,1)S(1)} %get-tuple-element.58), channel_id=1, source_target_pairs={{0,2},{1,3},{2,0},{3,1},{4,6},{5,7},{6,4},{7,5},{8,10},{9,11},{10,... | collective-permute-start | bytes 786440 | tf_op jit(solution)/shard_map/ppermute | solution.py:232
  121.6 0.8 copy.107
  122.5 0.8 copy.108
  123.3 0.3 reshape.144
  123.7 0.2 slice.330
  123.9 0.8 copy.109
  124.7 0.2 copy.106
  124.9 0.7 reshape.145
  125.5 1.0 slice_reduce_fusion
  126.5 0.8 collective-permute-done.2
  127.3 5.7 %collective-permute-done.1 = bf16[32,4096]{1,0:T(8,128)(2,1)S(1)} collective-permute-done((bf16[32,4096]{1,0:T(8,128)(2,1)S(1)}, bf16[32,4096]{1,0:T(8,128)(2,1)S(1)}, u32[]{:S(2)}, u32[]{:S(2)}) %collective-permute-start.1) | collective-permute-done | bytes 262176 | tf_op jit(solution)/shard_map/ppermute | solution.py:232
  133.0 0.8 add_convert_fusion
  (47 shorter events, 1.7 us)
Async XLA Ops:
  0.6 21.6 %copy-start = (f32[1024,3,3]{0,2,1:T(4,128)S(1)}, f32[1024,3,3]{0,2,1:T(4,128)}, u32[]{:S(2)}) copy-start(f32[1024,3,3]{0,2,1:T(4,128)} %param.14) | copy-start | bytes 110596
  6.6 44.2 %all-to-all-start = ((bf16[64,4,16,128]{3,2,1,0:T(8,128)(2,1)}), bf16[64,4,16,128]{3,2,1,0:T(8,128)(2,1)S(1)}, u32[]{:S(2)}, u32[]{:S(2)}) async-start(bf16[64,4,16,128]{3,2,1,0:T(8,128)(2,1)} %copy.91), calls=%async_computation | async-start | bytes 2097152 | tf_op jit(solution)/shard_map/all_to_all | solution.py:179
  73.3 30.2 %all-to-all-start.1 = ((bf16[64,3,16,128]{3,2,1,0:T(8,128)(2,1)}), bf16[64,3,16,128]{3,2,1,0:T(8,128)(2,1)S(1)}, u32[]{:S(2)}, u32[]{:S(2)}) async-start(bf16[64,3,16,128]{3,2,1,0:T(8,128)(2,1)} %copy.100), calls=%async_computation.1 | async-start | bytes 1572864 | tf_op jit(solution)/shard_map/all_to_all | solution.py:196
  104.4 18.9 %all-to-all-start.2 = ((f32[64,4,128]{2,1,0:T(4,128)}), f32[64,4,128]{2,1,0:T(4,128)S(1)}, u32[]{:S(2)}, u32[]{:S(2)}) async-start(f32[64,4,128]{2,1,0:T(4,128)} %broadcast_in_dim.18), calls=%async_computation.2 | async-start | bytes 262144 | tf_op jit(solution)/shard_map/all_to_all | solution.py:215
  118.5 8.0 %collective-permute-start = (bf16[32,4096]{1,0:T(8,128)(2,1)}, bf16[32,4096]{1,0:T(8,128)(2,1)S(1)}, u32[]{:S(2)}, u32[]{:S(2)}) collective-permute-start(bf16[32,4096]{1,0:T(8,128)(2,1)} %get-tuple-element.56), channel_id=1, source_target_pairs={{0,1},{1,2},{2,3},{3,0},{4,5},{5,6},{6,7},{7,4},{8,9},{9,10},{10,1... | collective-permute-start | bytes 786440 | tf_op jit(solution)/shard_map/ppermute | solution.py:232
  118.5 8.8 %collective-permute-start.2 = (bf16[32,4096]{1,0:T(8,128)(2,1)}, bf16[32,4096]{1,0:T(8,128)(2,1)S(1)}, u32[]{:S(2)}, u32[]{:S(2)}) collective-permute-start(bf16[32,4096]{1,0:T(8,128)(2,1)} %get-tuple-element.57), channel_id=1, source_target_pairs={{0,3},{1,0},{2,1},{3,2},{4,7},{5,4},{6,5},{7,6},{8,11},{9,8},{10,9... | collective-permute-start | bytes 786440 | tf_op jit(solution)/shard_map/ppermute | solution.py:232
  120.3 12.7 %collective-permute-start.1 = (bf16[32,4096]{1,0:T(8,128)(2,1)S(1)}, bf16[32,4096]{1,0:T(8,128)(2,1)S(1)}, u32[]{:S(2)}, u32[]{:S(2)}) collective-permute-start(bf16[32,4096]{1,0:T(8,128)(2,1)S(1)} %get-tuple-element.58), channel_id=1, source_target_pairs={{0,2},{1,3},{2,0},{3,1},{4,6},{5,7},{6,4},{7,5},{8,10},{9,11},{10,... | collective-permute-start | bytes 786440 | tf_op jit(solution)/shard_map/ppermute | solution.py:232
